TPU v7x, 32 devices: a whole 2x2x4 slice. The times are simulated.
32 devices in a mesh: wide: 16 (over z, y, x), narrow: 2 (over core).
Axes of the slice: x: 2, y: 2, z: 4, core: 2. Of those that a mesh axis runs over, the one named last changes fastest.
Arguments:
- features: float32 [2, 16, 512, 256], P('narrow', 'wide'), may hold values from -6 to 6
- out_grad: float32 [2, 16, 512, 256], P('narrow', 'wide'), may hold values from -0.06629126 to 0.06629126
- bank: float32 [4, 256, 2304], P(None, 'wide'), may hold values from -0.125 to 0.125
- mix_seed: int32 [16, 4], replicated, may hold values from 0 to 255
- style_of: int32 [2], P('narrow'), may hold values from 0 to 15
Outputs:
- bank_grad: float32 [4, 256, 2304], P(None, 'wide')
All inputs are finite; a program needn't handle non-finite values.
Results may differ from a plain program's by a relative error of at most 0.0001.
Values sent between devices are 32-bit elements; how exact they have to be, the bound alone decides.
No kernel may reach another device: no remote copies, remote signals or barrier semaphores. Data moves between devices by JAX's collectives and lax.ppermute only.
A program may use at most 64 MiB of HBM per device.

v0:
```python
import functools

import jax
import jax.numpy as jnp
from jax import lax
from jax.experimental import pallas as pl
from jax.experimental.pallas import tpu as pltpu
from jax.sharding import PartitionSpec as P


F32, BF16 = jnp.float32, jnp.bfloat16
VMEM_SPEC = pl.BlockSpec(memory_space=pltpu.VMEM)
SMEM_SPEC = pl.BlockSpec(memory_space=pltpu.SMEM)
ANY_SPEC = pl.BlockSpec(memory_space=pl.ANY)


def place():
    me = lax.axis_index("wide")
    return me // 4, me % 4, me % 2, (me // 2) % 2


def call(body, outs, ins, out_specs=None, flops=0, scratch=(), alias=None, limit=40 * 2**20):
    return pl.pallas_call(
        body,
        out_shape=outs,
        in_specs=[{"v": VMEM_SPEC, "s": SMEM_SPEC, "a": ANY_SPEC}[i] for i in ins],
        out_specs=jax.tree.map(lambda _: VMEM_SPEC, outs) if out_specs is None else out_specs,
        scratch_shapes=list(scratch),
        input_output_aliases=alias or {},
        compiler_params=pltpu.CompilerParams(vmem_limit_bytes=limit),
        cost_estimate=pl.CostEstimate(flops=flops, bytes_accessed=2**20, transcendentals=0),
    )


def features_body(f_ref, f_keep, f_send):
    _, _, _, y = place()
    half = f_keep.shape[1]
    f_send[...] = f_ref[0, 0, :, pl.ds(pl.multiple_of((1 - y) * half, half), half)]
    f_keep[...] = f_ref[0, 0, :, pl.ds(pl.multiple_of(y * half, half), half)]


def grads_body(owned, g_ref, seed_ref, style_ref, g_keep, g_send, mix):
    _, _, x, _ = place()
    at = lax.broadcasted_iota(jnp.int32, mix.shape, 0)
    tile = jnp.zeros(mix.shape, F32)
    for k in range(seed_ref.shape[0]):
        weight = seed_ref[k, style_ref[0]].astype(F32) / 128.0 + 0.25
        tile = jnp.where(at == k, weight, tile)
    mix[...] = tile
    turned = jnp.transpose(g_ref[0, 0])
    for k in range(turned.shape[0] // (2 * owned)):
        low = turned[2 * k * owned : (2 * k + 1) * owned]
        high = turned[(2 * k + 1) * owned : (2 * k + 2) * owned]
        rows = slice(k * owned, (k + 1) * owned)
        g_keep[rows] = jnp.where(x == 0, low, high)
        g_send[rows] = jnp.where(x == 0, high, low)


def mix_body(every_ref, bank_ref, f_in, g_in, mixed_ref, scale_ref, f_out, g_out):
    samples, kinds = every_ref.shape[0], bank_ref.shape[0]
    for s in range(samples):
        mixed = every_ref[s, 0:1, 0:1] * bank_ref[0]
        for k in range(1, kinds):
            mixed = mixed + every_ref[s, k : k + 1, 0:1] * bank_ref[k]
        mixed_ref[s] = mixed
        scale = lax.rsqrt(jnp.sum(mixed * mixed, axis=1, keepdims=True) + 1e-08)
        scale_ref[s] = jnp.broadcast_to(scale, scale_ref.shape[1:])


def split(v):
    high = v.astype(BF16)
    return high, (v - high.astype(F32)).astype(BF16)


def shifted(g):
    width = g.shape[1]
    at = lax.broadcasted_iota(jnp.int32, g.shape, 1)
    ahead = jnp.where(at == width - 1, 0.0, pltpu.roll(g, width - 1, 1))
    behind = jnp.where(at == 0, 0.0, pltpu.roll(g, 1, 1))
    return split(jnp.concatenate([ahead, g, behind], axis=0))


def product(left_high, left_low, right, half):
    both = jnp.dot(left_high, right, preferred_element_type=F32)
    return (
        both[:, :half]
        + both[:, half:]
        + jnp.dot(left_low, right[:, :half], preferred_element_type=F32)
    )


def operands(f, g, lh, ll, rt):
    half = f.shape[1]
    lh[...], ll[...] = shifted(g[...])
    high, low = split(f[...])
    rt[:, :half] = high
    rt[:, half:] = low


def near_body(*refs):
    fs, gs, acc, lh, ll, rt = refs[0:3], refs[3:6], *refs[6:]
    _, _, x, _ = place()
    half = fs[0].shape[1]
    for role in range(3):
        operands(fs[role], gs[role], lh.at[role], ll.at[role], rt.at[role])

    def mul(a, b):
        return product(lh[a], ll[a], rt[b], half)

    up = jnp.where(x == 0, 2, 0)
    acc[1] = mul(0, 0) + mul(1, 1) + mul(2, 2)
    acc[up] = mul(0, 1)
    acc[2 - up] = mul(1, 0)


def far_body(f, g, acc_in, lh, ll, rt, acc, lh_far, ll_far, rt_far):
    _, _, x, y = place()
    half = f.shape[1]
    operands(f, g, lh_far, ll_far, rt_far)
    far = (lh_far, ll_far, rt_far)
    own, xn, yn = [(lh.at[i], ll.at[i], rt.at[i]) for i in range(3)]

    def mul(a, b):
        return product(a[0][...], a[1][...], b[2][...], half)

    up = jnp.where(x == 0, 2, 0)
    acc[1] = acc_in[1] + mul(far, far)
    acc[up] = acc_in[up] + mul(yn, far)
    acc[2 - up] = acc_in[2 - up] + mul(far, yn)
    onward = jnp.where(y == 0, 2, 0)

    def middle(a, b):
        acc[onward] += mul(a, b)
        acc[2 - onward] += mul(b, a)

    pl.when(x == y)(lambda: middle(xn, yn))
    pl.when(x != y)(lambda: middle(own, far))


def edge_body(groups, owned, *refs):
    fe, ge, acc_in, lh, ll, rt, lh_far, ll_far, rt_far = refs[:9]
    outs, acc, lh_ex, ll_ex, rt_ex = refs[9:-4], *refs[-4:]
    group, _, x, y = place()
    half = fe.shape[1]
    operands(fe, ge, lh_ex, ll_ex, rt_ex)
    up = jnp.where(x == 0, 2, 0)
    acc[1] = acc_in[1]

    def outer(lh_in, ll_in, rt_in):
        acc[up] = acc_in[up] + product(lh_in[...], ll_in[...], rt_ex[...], half)
        acc[2 - up] = acc_in[2 - up] + product(lh_ex[...], ll_ex[...], rt_in[...], half)

    pl.when(x == y)(lambda: outer(lh_far, ll_far, rt_far))
    pl.when(x != y)(lambda: outer(lh.at[1], ll.at[1], rt.at[1]))
    n_out = ge.shape[0]
    rows = 2 * owned
    for m in range(groups):
        start = pl.multiple_of((group ^ m) * rows, rows)
        for a in range(3):
            for b in range(3):
                both = acc[a, pl.ds(b * n_out + start, rows), :]
                low, high = both[:owned], both[owned:]
                outs[2 * m][3 * a + b] = jnp.where(y == 0, low, high)
                outs[2 * m + 1][3 * a + b] = jnp.where(y == 0, high, low)


def sum_body(*refs):
    parts, out = refs[:-1], refs[-1]
    taps = parts[0].shape[0]
    for d in range(2):
        for t in range(taps):
            total = parts[d][t]
            for part in parts[d + 2 :: 2]:
                total = total + part[t]
            out[0, d * taps + t] = total


def final_body(sums_ref, every_ref, mixed_ref, scale_ref, out_ref, held, sem):
    _, _, _, y = place()
    samples, taps = sums_ref.shape[0], sums_ref.shape[1] // 2
    kinds = held.shape[0]
    grads = []
    for s in range(samples):
        pieces = []
        for t in range(taps):
            kept, got = sums_ref[s, t], sums_ref[s, taps + t]
            pieces += [jnp.where(y == 0, kept, got), jnp.where(y == 0, got, kept)]
        grad = jnp.concatenate(pieces, axis=1)
        mixed, scale = mixed_ref[s], scale_ref[s, :, 0:1]
        inner = jnp.sum(mixed * grad, axis=1, keepdims=True)
        grads.append(scale * grad - (scale * scale * scale * inner) * mixed)
    copies = []
    for k in range(kinds):
        total = every_ref[0, k : k + 1, 0:1] * grads[0]
        for s in range(1, samples):
            total = total + every_ref[s, k : k + 1, 0:1] * grads[s]
        held[k] = total
        copies.append(pltpu.make_async_copy(held.at[k], out_ref.at[k], sem.at[k]))
        copies[-1].start()
    for copy in copies:
        copy.wait()


def send(value, pairs):
    return lax.ppermute(value, "wide", pairs)


def local(features, out_grad, bank, mix_seed, style_of):
    size = lax.axis_size("wide")
    groups = size // 4
    _, _, map_width, in_channels = features.shape
    out_channels = out_grad.shape[3]
    owned = bank.shape[1]
    half_in, half_out = in_channels // 2, out_channels // 2
    everyone = range(size)
    over_x = [(i, i ^ 1) for i in everyone]
    over_y = [(i, i ^ 2) for i in everyone]
    outward = [(i, i + 4 if i % 2 else i - 4) for i in everyone]
    outward = [(i, j) for i, j in outward if 0 <= j < size]

    def shape(*dims, dtype=F32):
        return jax.ShapeDtypeStruct(dims, dtype)

    f_shape, g_shape = shape(map_width, half_in), shape(half_out, map_width)
    mix_shape = shape(owned, 128)
    f_keep, f_send = call(features_body, (f_shape, f_shape), "v")(features)
    g_keep, g_send, mix = call(
        functools.partial(grads_body, owned), (g_shape, g_shape, mix_shape), "vss"
    )(out_grad, mix_seed.T, style_of)

    f_yn = send(f_send, over_y)
    g_xn = send(g_send, over_x)
    every_mix = lax.all_gather(mix[None], "narrow", axis=0, tiled=True)
    samples = every_mix.shape[0]
    mixed, scale, f_keep, g_keep = call(
        mix_body,
        (shape(samples, *bank.shape[1:]), shape(samples, owned, 128), f_shape, g_shape),
        "vvaa",
        (VMEM_SPEC, VMEM_SPEC, ANY_SPEC, ANY_SPEC),
        alias={2: 2, 3: 3},
    )(every_mix, bank, f_keep, g_keep)
    f_xn = send(f_keep, over_x)
    g_yn = send(g_keep, over_y)
    f_dg = send(f_yn, over_x)
    g_dg = send(g_xn, over_y)
    me = lax.axis_index("wide")
    same = (me % 2) == ((me // 2) % 2)
    f_ex = send(jnp.where(same, f_keep, f_yn), outward)
    g_ex = send(jnp.where(same, g_keep, g_yn), outward)

    pair = 2 * 3 * 3 * half_out * half_in * map_width
    sums = shape(3, 3 * half_out, half_in)
    left = shape(3 * half_out, map_width, dtype=BF16)
    right = shape(map_width, 2 * half_in, dtype=BF16)
    lefts = shape(3, *left.shape, dtype=BF16)
    rights = shape(3, *right.shape, dtype=BF16)
    acc, *near = call(near_body, (sums, lefts, lefts, rights), "v" * 6, flops=5 * pair)(
        f_keep, f_xn, f_yn, g_keep, g_xn, g_yn
    )
    acc, *far = call(far_body, (sums, left, left, right), "v" * 6, flops=5 * pair)(
        f_dg, g_dg, acc, *near
    )
    piece = shape(9, owned, half_in)
    blocks = call(
        functools.partial(edge_body, groups, owned),
        [piece] * (2 * groups),
        "v" * 9,
        flops=2 * pair,
        scratch=[pltpu.VMEM(a.shape, a.dtype) for a in (sums, left, left, right)],
    )(f_ex, g_ex, acc, *near, *far)
    parts = [blocks[0]] + [
        send(blocks[n], [(i, i ^ (2 * n)) for i in everyone])
        for n in range(1, 2 * groups)
    ]
    own_sums = call(sum_body, shape(1, 18, owned, half_in), "v" * (2 * groups))(
        *parts
    )
    every_sum = lax.all_gather(own_sums, "narrow", axis=0, tiled=True)
    return call(
        final_body,
        shape(*bank.shape),
        "vvvv",
        ANY_SPEC,
        scratch=(pltpu.VMEM(bank.shape, F32), pltpu.SemaphoreType.DMA((bank.shape[0],))),
    )(every_sum, every_mix, mixed, scale)


def solution(mesh):
    placed = (
        P("narrow", "wide", None, None),
        P("narrow", "wide", None, None),
        P(None, "wide", None),
        P(),
        P("narrow"),
    )
    return jax.shard_map(
        local, mesh=mesh, in_specs=placed, out_specs=P(None, "wide", None), check_vma=False
    )
```

profile of v0, /device:TPU:0, one launch (start us, length us, event | category | flops | bytes accessed | tf_op | source)
XLA Modules:
  0.0 49.4 jit_solution(10900537246811194394)
XLA Ops:
  0.0 1.0 %copy-done.2 = f32[1,1,512,256]{3,2,1,0:T(8,128)S(1)} copy-done((f32[1,1,512,256]{3,2,1,0:T(8,128)S(1)}, f32[1,1,512,256]{3,2,1,0:T(8,128)}, u32[]{:S(2)}) %copy-start.2) | copy-done | bytes 524312
  1.1 3.1 %collective-permute-start = (f32[512,128]{1,0:T(8,128)S(1)}, f32[512,128]{1,0:T(8,128)S(1)}, u32[]{:S(2)}, u32[]{:S(2)}) collective-permute-start(f32[512,128]{1,0:T(8,128)S(1)} %get-tuple-element.34), channel_id=1, source_target_pairs={{0,4},{2,6},{4,0},{6,2},{8,12},{10,14},{12,8},{14,10},{16,20},{18,... | collective-permute-start | bytes 786440 | tf_op jit(solution)/shard_map/ppermute | solution.py:205
  4.8 1.0 %copy-done.1 = f32[1,1,512,256]{3,2,1,0:T(8,128)S(1)} copy-done((f32[1,1,512,256]{3,2,1,0:T(8,128)S(1)}, f32[1,1,512,256]{3,2,1,0:T(8,128)}, u32[]{:S(2)}) %copy-start.1) | copy-done | bytes 524312
  7.3 1.6 %collective-permute-start.5 = (f32[128,512]{1,0:T(8,128)S(1)}, f32[128,512]{1,0:T(8,128)S(1)}, u32[]{:S(2)}, u32[]{:S(2)}) collective-permute-start(f32[128,512]{1,0:T(8,128)S(1)} %get-tuple-element.36), channel_id=1, source_target_pairs={{0,2},{2,0},{4,6},{6,4},{8,10},{10,8},{12,14},{14,12},{16,18},{18,... | collective-permute-start | bytes 786440 | tf_op jit(solution)/shard_map/ppermute | solution.py:205
  8.8 1.8 %all-gather = f32[32,128]{1,0:T(8,128)S(1)} all-gather(f32[16,128]{1,0:T(8,128)S(1)} %get-tuple-element.30), channel_id=2, replica_groups=mesh['wide'=16,'narrow'=2] {'narrow'}, dimensions={0}, use_global_device_ids=true | all-gather | bytes 24576 | tf_op jit(solution)/shard_map/all_gather | solution.py:233
  11.5 1.3 %collective-permute-start.1 = (f32[512,128]{1,0:T(8,128)S(1)}, f32[512,128]{1,0:T(8,128)S(1)}, u32[]{:S(2)}, u32[]{:S(2)}) collective-permute-start(f32[512,128]{1,0:T(8,128)S(1)} %broadcast_select_fusion.1), channel_id=1, source_target_pairs={{2,10},{6,14},{8,0},{10,18},{12,4},{14,22},{16,8},{18,26},{20,12},... | collective-permute-start | bytes 786440 | tf_op jit(solution)/shard_map/ppermute | solution.py:205
  12.8 4.2 %collective-permute-start.4 = (f32[512,128]{1,0:T(8,128)S(1)}, f32[512,128]{1,0:T(8,128)S(1)}, u32[]{:S(2)}, u32[]{:S(2)}) collective-permute-start(f32[512,128]{1,0:T(8,128)S(1)} %collective-permute-done.refs_2_), channel_id=1, source_target_pairs={{0,2},{2,0},{4,6},{6,4},{8,10},{10,8},{12,14},{14,12},{16,18},{18,... | collective-permute-start | bytes 786440 | tf_op jit(solution)/shard_map/ppermute | solution.py:205
  17.0 1.5 %collective-permute-start.6 = (f32[128,512]{1,0:T(8,128)S(1)}, f32[128,512]{1,0:T(8,128)S(1)}, u32[]{:S(2)}, u32[]{:S(2)}) collective-permute-start(f32[128,512]{1,0:T(8,128)S(1)} %collective-permute-done.5.refs_4_), channel_id=1, source_target_pairs={{0,4},{2,6},{4,0},{6,2},{8,12},{10,14},{12,8},{14,10},{16,20},{18,... | collective-permute-start | bytes 786440 | tf_op jit(solution)/shard_map/ppermute | solution.py:205
  18.6 1.3 %collective-permute-done.2.refs_5_ = f32[128,512]{1,0:T(8,128)S(1)} collective-permute-done((f32[128,512]{1,0:T(8,128)S(1)}, f32[128,512]{1,0:T(8,128)S(1)}, u32[]{:S(2)}, u32[]{:S(2)}) %collective-permute-start.2) | collective-permute-done | bytes 262176 | tf_op jit(solution)/shard_map/ppermute | solution.py:205
  19.9 1.3 %collective-permute-start.3 = (f32[128,512]{1,0:T(8,128)S(1)}, f32[128,512]{1,0:T(8,128)S(1)}, u32[]{:S(2)}, u32[]{:S(2)}) collective-permute-start(f32[128,512]{1,0:T(8,128)S(1)} %broadcast_select_fusion), channel_id=1, source_target_pairs={{2,10},{6,14},{8,0},{10,18},{12,4},{14,22},{16,8},{18,26},{20,12},... | collective-permute-start | bytes 786440 | tf_op jit(solution)/shard_map/ppermute | solution.py:205
  22.0 1.3 %shard_map.58 = (f32[3,384,128]{2,1,0:T(8,128)S(1)}, bf16[3,384,512]{2,1,0:T(8,128)(2,1)S(1)}, bf16[3,384,512]{2,1,0:T(8,128)(2,1)S(1)}, bf16[3,512,256]{2,1,0:T(8,128)(2,1)S(1)}) custom-call(f32[512,128]{1,0:T(8,128)S(1)} %get-tuple-element.33.refs_0_, f32[512,128]{1,0:T(8,128)S(1)} %collective-permute-done.7.refs_1_, ...), custom_call_target="tpu_custom_call" | custom-call | flops 754974720 | bytes 1048576 | tf_op jit(solution)/shard_map/pallas_call | solution.py:257
  23.3 3.0 %collective-permute-done.4.f = f32[512,128]{1,0:T(8,128)S(1)} collective-permute-done((f32[512,128]{1,0:T(8,128)S(1)}, f32[512,128]{1,0:T(8,128)S(1)}, u32[]{:S(2)}, u32[]{:S(2)}) %collective-permute-start.4) | collective-permute-done | bytes 262176 | tf_op jit(solution)/shard_map/ppermute | solution.py:205
  26.4 1.4 %shard_map.59 = (f32[3,384,128]{2,1,0:T(8,128)S(1)}, bf16[384,512]{1,0:T(8,128)(2,1)S(1)}, bf16[384,512]{1,0:T(8,128)(2,1)S(1)}, bf16[512,256]{1,0:T(8,128)(2,1)S(1)}) custom-call(f32[512,128]{1,0:T(8,128)S(1)} %collective-permute-done.4.f, f32[128,512]{1,0:T(8,128)S(1)} %collective-permute-done.6.g, f32[3,384,128]{2,1,0:T(8,128)S(1)} %get-tuple-element.37.acc_in, ...), custom_call_target="tpu_custom_call" | custom-call | flops 754974720 | bytes 1048576 | tf_op jit(solution)/shard_map/pallas_call | solution.py:260
  27.8 0.9 %collective-permute-done.3.refs_1_ = f32[128,512]{1,0:T(8,128)S(1)} collective-permute-done((f32[128,512]{1,0:T(8,128)S(1)}, f32[128,512]{1,0:T(8,128)S(1)}, u32[]{:S(2)}, u32[]{:S(2)}) %collective-permute-start.3) | collective-permute-done | bytes 262176 | tf_op jit(solution)/shard_map/ppermute | solution.py:205
  28.7 0.9 %shard_map.60 = (f32[9,16,128]{2,1,0:T(8,128)S(1)}, f32[9,16,128]{2,1,0:T(8,128)S(1)}, f32[9,16,128]{2,1,0:T(8,128)S(1)}, f32[9,16,128]{2,1,0:T(8,128)S(1)}, f32...) custom-call(f32[512,128]{1,0:T(8,128)S(1)} %collective-permute-done.1, ...), custom_call_target="tpu_custom_call" | custom-call | flops 301989888 | bytes 1048576 | tf_op jit(solution)/shard_map/pallas_call | solution.py:264
  30.2 1.6 %collective-permute-start.9 = (f32[9,16,128]{2,1,0:T(8,128)S(1)}, f32[9,16,128]{2,1,0:T(8,128)S(1)}, u32[]{:S(2)}, u32[]{:S(2)}) collective-permute-start(f32[9,16,128]{2,1,0:T(8,128)S(1)} %get-tuple-element.47), channel_id=1, source_target_pairs={{0,8},{2,10},{4,12},{6,14},{8,0},{10,2},{12,4},{14,6},{16,24},{18,... | collective-permute-start | bytes 221192 | tf_op jit(solution)/shard_map/ppermute | solution.py:205
  31.7 1.4 %collective-permute-start.10 = (f32[9,16,128]{2,1,0:T(8,128)S(1)}, f32[9,16,128]{2,1,0:T(8,128)S(1)}, u32[]{:S(2)}, u32[]{:S(2)}) collective-permute-start(f32[9,16,128]{2,1,0:T(8,128)S(1)} %get-tuple-element.48), channel_id=1, source_target_pairs={{0,12},{2,14},{4,8},{6,10},{8,4},{10,6},{12,0},{14,2},{16,28},{18,... | collective-permute-start | bytes 221192 | tf_op jit(solution)/shard_map/ppermute | solution.py:205
  33.2 2.6 %collective-permute-start.11 = (f32[9,16,128]{2,1,0:T(8,128)S(1)}, f32[9,16,128]{2,1,0:T(8,128)S(1)}, u32[]{:S(2)}, u32[]{:S(2)}) collective-permute-start(f32[9,16,128]{2,1,0:T(8,128)S(1)} %get-tuple-element.49), channel_id=1, source_target_pairs={{0,16},{2,18},{4,20},{6,22},{8,24},{10,26},{12,28},{14,30},{16,0},... | collective-permute-start | bytes 221192 | tf_op jit(solution)/shard_map/ppermute | solution.py:205
  36.0 2.7 %collective-permute-start.13 = (f32[9,16,128]{2,1,0:T(8,128)S(1)}, f32[9,16,128]{2,1,0:T(8,128)S(1)}, u32[]{:S(2)}, u32[]{:S(2)}) collective-permute-start(f32[9,16,128]{2,1,0:T(8,128)S(1)} %get-tuple-element.51), channel_id=1, source_target_pairs={{0,24},{2,26},{4,28},{6,30},{8,16},{10,18},{12,20},{14,22},{16,8},... | collective-permute-start | bytes 221192 | tf_op jit(solution)/shard_map/ppermute | solution.py:205
  38.8 2.0 %collective-permute-start.14 = (f32[9,16,128]{2,1,0:T(8,128)S(1)}, f32[9,16,128]{2,1,0:T(8,128)S(1)}, u32[]{:S(2)}, u32[]{:S(2)}) collective-permute-start(f32[9,16,128]{2,1,0:T(8,128)S(1)} %get-tuple-element.52), channel_id=1, source_target_pairs={{0,28},{2,30},{4,24},{6,26},{8,20},{10,22},{12,16},{14,18},{16,12}... | collective-permute-start | bytes 221192 | tf_op jit(solution)/shard_map/ppermute | solution.py:205
  40.8 3.0 %collective-permute-done.11.refs_4_ = f32[9,16,128]{2,1,0:T(8,128)S(1)} collective-permute-done((f32[9,16,128]{2,1,0:T(8,128)S(1)}, f32[9,16,128]{2,1,0:T(8,128)S(1)}, u32[]{:S(2)}, u32[]{:S(2)}) %collective-permute-start.11) | collective-permute-done | bytes 73760 | tf_op jit(solution)/shard_map/ppermute | solution.py:205
  43.9 2.4 %collective-permute-done.12.refs_5_ = f32[9,16,128]{2,1,0:T(8,128)S(1)} collective-permute-done((f32[9,16,128]{2,1,0:T(8,128)S(1)}, f32[9,16,128]{2,1,0:T(8,128)S(1)}, u32[]{:S(2)}, u32[]{:S(2)}) %collective-permute-start.12) | collective-permute-done | bytes 73760 | tf_op jit(solution)/shard_map/ppermute | solution.py:205
  46.3 2.0 %all_gather.7.sums_ref = f32[2,18,16,128]{3,2,1,0:T(8,128)S(1)} all-gather(f32[1,18,16,128]{3,2,1,0:T(8,128)S(1)} %shard_map.61), channel_id=1, replica_groups=mesh['wide'=16,'narrow'=2] {'narrow'}, dimensions={0}, use_global_device_ids=true | all-gather | bytes 442368 | tf_op jit(solution)/shard_map/all_gather | solution.py:278
  48.3 1.1 %shard_map.62 = f32[4,16,2304]{2,1,0:T(8,128)} custom-call(f32[2,18,16,128]{3,2,1,0:T(8,128)S(1)} %all_gather.7.sums_ref, f32[2,16,128]{2,1,0:T(8,128)S(1)} %bitcast.3, f32[2,16,2304]{2,1,0:T(8,128)S(1)} %get-tuple-element.53.mixed_ref, f32[2,16,128]{2,1,0:T(8,128)S(1)} %get-tuple-element.54.scale_ref), custom_call_target="tpu_custom_call" | custom-call | bytes 1048576 | tf_op jit(solution)/shard_map/pallas_call | solution.py:279
  (26 shorter events, 4.1 us)
Async XLA Ops:
  0.0 1.0 %copy-start.2 = (f32[1,1,512,256]{3,2,1,0:T(8,128)S(1)}, f32[1,1,512,256]{3,2,1,0:T(8,128)}, u32[]{:S(2)}) copy-start(f32[1,1,512,256]{3,2,1,0:T(8,128)} %f_ref.1) | copy-start | bytes 1572868
  1.0 9.6 %copy-start = (f32[4,16,2304]{2,1,0:T(8,128)S(1)}, f32[4,16,2304]{2,1,0:T(8,128)}, u32[]{:S(2)}) copy-start(f32[4,16,2304]{2,1,0:T(8,128)} %bank_ref.1) | copy-start | bytes 1769476
  1.1 10.4 %collective-permute-start = (f32[512,128]{1,0:T(8,128)S(1)}, f32[512,128]{1,0:T(8,128)S(1)}, u32[]{:S(2)}, u32[]{:S(2)}) collective-permute-start(f32[512,128]{1,0:T(8,128)S(1)} %get-tuple-element.34), channel_id=1, source_target_pairs={{0,4},{2,6},{4,0},{6,2},{8,12},{10,14},{12,8},{14,10},{16,20},{18,... | collective-permute-start | bytes 786440 | tf_op jit(solution)/shard_map/ppermute | solution.py:205
  4.8 1.0 %copy-start.1 = (f32[1,1,512,256]{3,2,1,0:T(8,128)S(1)}, f32[1,1,512,256]{3,2,1,0:T(8,128)}, u32[]{:S(2)}) copy-start(f32[1,1,512,256]{3,2,1,0:T(8,128)} %g_ref.1) | copy-start | bytes 1572868
  5.8 0.7 %copy-start.3 = (s32[16,4]{0,1:T(4,128)S(1)}, s32[16,4]{0,1:T(4,128)}, u32[]{:S(2)}) copy-start(s32[16,4]{0,1:T(4,128)} %param.8) | copy-start | bytes 772
  7.3 9.7 %collective-permute-start.5 = (f32[128,512]{1,0:T(8,128)S(1)}, f32[128,512]{1,0:T(8,128)S(1)}, u32[]{:S(2)}, u32[]{:S(2)}) collective-permute-start(f32[128,512]{1,0:T(8,128)S(1)} %get-tuple-element.36), channel_id=1, source_target_pairs={{0,2},{2,0},{4,6},{6,4},{8,10},{10,8},{12,14},{14,12},{16,18},{18,... | collective-permute-start | bytes 786440 | tf_op jit(solution)/shard_map/ppermute | solution.py:205
  10.9 9.0 %collective-permute-start.2 = (f32[128,512]{1,0:T(8,128)S(1)}, f32[128,512]{1,0:T(8,128)S(1)}, u32[]{:S(2)}, u32[]{:S(2)}) collective-permute-start(f32[128,512]{1,0:T(8,128)S(1)} %get-tuple-element.35.refs_3_), channel_id=1, source_target_pairs={{0,4},{2,6},{4,0},{6,2},{8,12},{10,14},{12,8},{14,10},{16,20},{18,... | collective-permute-start | bytes 786440 | tf_op jit(solution)/shard_map/ppermute | solution.py:205
  11.4 10.6 %collective-permute-start.7 = (f32[512,128]{1,0:T(8,128)S(1)}, f32[512,128]{1,0:T(8,128)S(1)}, u32[]{:S(2)}, u32[]{:S(2)}) collective-permute-start(f32[512,128]{1,0:T(8,128)S(1)} %get-tuple-element.33.refs_0_), channel_id=1, source_target_pairs={{0,2},{2,0},{4,6},{6,4},{8,10},{10,8},{12,14},{14,12},{16,18},{18,... | collective-permute-start | bytes 786440 | tf_op jit(solution)/shard_map/ppermute | solution.py:205
  11.5 16.3 %collective-permute-start.1 = (f32[512,128]{1,0:T(8,128)S(1)}, f32[512,128]{1,0:T(8,128)S(1)}, u32[]{:S(2)}, u32[]{:S(2)}) collective-permute-start(f32[512,128]{1,0:T(8,128)S(1)} %broadcast_select_fusion.1), channel_id=1, source_target_pairs={{2,10},{6,14},{8,0},{10,18},{12,4},{14,22},{16,8},{18,26},{20,12},... | collective-permute-start | bytes 786440 | tf_op jit(solution)/shard_map/ppermute | solution.py:205
  12.8 13.5 %collective-permute-start.4 = (f32[512,128]{1,0:T(8,128)S(1)}, f32[512,128]{1,0:T(8,128)S(1)}, u32[]{:S(2)}, u32[]{:S(2)}) collective-permute-start(f32[512,128]{1,0:T(8,128)S(1)} %collective-permute-done.refs_2_), channel_id=1, source_target_pairs={{0,2},{2,0},{4,6},{6,4},{8,10},{10,8},{12,14},{14,12},{16,18},{18,... | collective-permute-start | bytes 786440 | tf_op jit(solution)/shard_map/ppermute | solution.py:205
  17.0 9.3 %collective-permute-start.6 = (f32[128,512]{1,0:T(8,128)S(1)}, f32[128,512]{1,0:T(8,128)S(1)}, u32[]{:S(2)}, u32[]{:S(2)}) collective-permute-start(f32[128,512]{1,0:T(8,128)S(1)} %collective-permute-done.5.refs_4_), channel_id=1, source_target_pairs={{0,4},{2,6},{4,0},{6,2},{8,12},{10,14},{12,8},{14,10},{16,20},{18,... | collective-permute-start | bytes 786440 | tf_op jit(solution)/shard_map/ppermute | solution.py:205
  19.9 8.8 %collective-permute-start.3 = (f32[128,512]{1,0:T(8,128)S(1)}, f32[128,512]{1,0:T(8,128)S(1)}, u32[]{:S(2)}, u32[]{:S(2)}) collective-permute-start(f32[128,512]{1,0:T(8,128)S(1)} %broadcast_select_fusion), channel_id=1, source_target_pairs={{2,10},{6,14},{8,0},{10,18},{12,4},{14,22},{16,8},{18,26},{20,12},... | collective-permute-start | bytes 786440 | tf_op jit(solution)/shard_map/ppermute | solution.py:205
  29.6 6.4 %collective-permute-start.8 = (f32[9,16,128]{2,1,0:T(8,128)S(1)}, f32[9,16,128]{2,1,0:T(8,128)S(1)}, u32[]{:S(2)}, u32[]{:S(2)}) collective-permute-start(f32[9,16,128]{2,1,0:T(8,128)S(1)} %get-tuple-element.46), channel_id=1, source_target_pairs={{0,4},{2,6},{4,0},{6,2},{8,12},{10,14},{12,8},{14,10},{16,20},{18,... | collective-permute-start | bytes 221192 | tf_op jit(solution)/shard_map/ppermute | solution.py:205
  30.2 8.6 %collective-permute-start.9 = (f32[9,16,128]{2,1,0:T(8,128)S(1)}, f32[9,16,128]{2,1,0:T(8,128)S(1)}, u32[]{:S(2)}, u32[]{:S(2)}) collective-permute-start(f32[9,16,128]{2,1,0:T(8,128)S(1)} %get-tuple-element.47), channel_id=1, source_target_pairs={{0,8},{2,10},{4,12},{6,14},{8,0},{10,2},{12,4},{14,6},{16,24},{18,... | collective-permute-start | bytes 221192 | tf_op jit(solution)/shard_map/ppermute | solution.py:205
  31.7 9.1 %collective-permute-start.10 = (f32[9,16,128]{2,1,0:T(8,128)S(1)}, f32[9,16,128]{2,1,0:T(8,128)S(1)}, u32[]{:S(2)}, u32[]{:S(2)}) collective-permute-start(f32[9,16,128]{2,1,0:T(8,128)S(1)} %get-tuple-element.48), channel_id=1, source_target_pairs={{0,12},{2,14},{4,8},{6,10},{8,4},{10,6},{12,0},{14,2},{16,28},{18,... | collective-permute-start | bytes 221192 | tf_op jit(solution)/shard_map/ppermute | solution.py:205
  33.2 10.7 %collective-permute-start.11 = (f32[9,16,128]{2,1,0:T(8,128)S(1)}, f32[9,16,128]{2,1,0:T(8,128)S(1)}, u32[]{:S(2)}, u32[]{:S(2)}) collective-permute-start(f32[9,16,128]{2,1,0:T(8,128)S(1)} %get-tuple-element.49), channel_id=1, source_target_pairs={{0,16},{2,18},{4,20},{6,22},{8,24},{10,26},{12,28},{14,30},{16,0},... | collective-permute-start | bytes 221192 | tf_op jit(solution)/shard_map/ppermute | solution.py:205
  35.7 10.5 %collective-permute-start.12 = (f32[9,16,128]{2,1,0:T(8,128)S(1)}, f32[9,16,128]{2,1,0:T(8,128)S(1)}, u32[]{:S(2)}, u32[]{:S(2)}) collective-permute-start(f32[9,16,128]{2,1,0:T(8,128)S(1)} %get-tuple-element.50), channel_id=1, source_target_pairs={{0,20},{2,22},{4,16},{6,18},{8,28},{10,30},{12,24},{14,26},{16,4},... | collective-permute-start | bytes 221192 | tf_op jit(solution)/shard_map/ppermute | solution.py:205
  36.0 10.2 %collective-permute-start.13 = (f32[9,16,128]{2,1,0:T(8,128)S(1)}, f32[9,16,128]{2,1,0:T(8,128)S(1)}, u32[]{:S(2)}, u32[]{:S(2)}) collective-permute-start(f32[9,16,128]{2,1,0:T(8,128)S(1)} %get-tuple-element.51), channel_id=1, source_target_pairs={{0,24},{2,26},{4,28},{6,30},{8,16},{10,18},{12,20},{14,22},{16,8},... | collective-permute-start | bytes 221192 | tf_op jit(solution)/shard_map/ppermute | solution.py:205
  38.8 7.5 %collective-permute-start.14 = (f32[9,16,128]{2,1,0:T(8,128)S(1)}, f32[9,16,128]{2,1,0:T(8,128)S(1)}, u32[]{:S(2)}, u32[]{:S(2)}) collective-permute-start(f32[9,16,128]{2,1,0:T(8,128)S(1)} %get-tuple-element.52), channel_id=1, source_target_pairs={{0,28},{2,30},{4,24},{6,26},{8,20},{10,22},{12,16},{14,18},{16,12}... | collective-permute-start | bytes 221192 | tf_op jit(solution)/shard_map/ppermute | solution.py:205
where the time goes:
time: 49.7 us; the launch traced here: 49.4 us
  starting transfers between devices  24.7 us (50%)
  waiting for transfers between devices  11.5 us (23%)
  Pallas kernels  5.8 us (12%)
  blocking collectives  3.82 us (8%)
  local copies, waits for them, and re-layouts  2.76 us (6%)
  between operations  0.75 us (2%)
    ppermute x15, starting transfers between devices, send(): return lax.ppermute(value, 'wide', pairs)  24.7 us
    ppermute x15, waiting for transfers between devices, send(): return lax.ppermute(value, 'wide', pairs)  11.5 us
    unnamed x8, local copies, waits for them, and re-layouts  2.76 us
    all_gather x1, blocking collectives, local(): every_sum = lax.all_gather(own_sums, 'narrow', axis=0, tiled=True)  2.02 us
    all_gather x1, blocking collectives, local(): every_mix = lax.all_gather(mix[None], 'narrow', axis=0, tiled=True)  1.81 us
    pallas_call x1, Pallas kernels, local(): call(far_body, (sums, left, left, right), 'v' * 6, flops=5 * pair)  1.45 us
    pallas_call x1, Pallas kernels, local(): call(near_body, (sums, lefts, lefts, rights), 'v' * 6, flops=5 * pair)  1.33 us
    pallas_call x1, Pallas kernels, local(): call(final_body, shape(*bank.shape), 'vvvv', ANY_SPEC, scratch=(pltpu.VME...  1.1 us
  transfers between devices with their start and end apart: 15, of which 6 were waited for; matrix products, arithmetic and copies ran while one was open for 0% of the time, Pallas kernels for 8%

commit v1 on v0

--- a/solution.py
+++ b/solution.py
@@ -39,14 +39,17 @@
     f_keep[...] = f_ref[0, 0, :, pl.ds(pl.multiple_of(y * half, half), half)]
 
 
-def grads_body(owned, g_ref, seed_ref, style_ref, g_keep, g_send, mix):
-    _, _, x, _ = place()
+def weights_body(seed_ref, style_ref, after_ref, mix):
     at = lax.broadcasted_iota(jnp.int32, mix.shape, 0)
     tile = jnp.zeros(mix.shape, F32)
     for k in range(seed_ref.shape[0]):
         weight = seed_ref[k, style_ref[0]].astype(F32) / 128.0 + 0.25
         tile = jnp.where(at == k, weight, tile)
     mix[...] = tile
+
+
+def grads_body(owned, g_ref, g_keep, g_send):
+    _, _, x, _ = place()
     turned = jnp.transpose(g_ref[0, 0])
     for k in range(turned.shape[0] // (2 * owned)):
         low = turned[2 * k * owned : (2 * k + 1) * owned]
@@ -143,6 +146,13 @@
     group, _, x, y = place()
     half = fe.shape[1]
     operands(fe, ge, lh_ex, ll_ex, rt_ex)
+
+    @pl.when(group == jnp.where(x == 1, 0, groups - 1))
+    def _():
+        lh_ex[...] = jnp.zeros_like(lh_ex)
+        ll_ex[...] = jnp.zeros_like(ll_ex)
+        rt_ex[...] = jnp.zeros_like(rt_ex)
+
     up = jnp.where(x == 0, 2, 0)
     acc[1] = acc_in[1]
 
@@ -215,18 +225,16 @@
     everyone = range(size)
     over_x = [(i, i ^ 1) for i in everyone]
     over_y = [(i, i ^ 2) for i in everyone]
-    outward = [(i, i + 4 if i % 2 else i - 4) for i in everyone]
-    outward = [(i, j) for i, j in outward if 0 <= j < size]
+    outward = [(i, (i + 4 if i % 2 else i - 4) % size) for i in everyone]
 
     def shape(*dims, dtype=F32):
         return jax.ShapeDtypeStruct(dims, dtype)
 
     f_shape, g_shape = shape(map_width, half_in), shape(half_out, map_width)
     mix_shape = shape(owned, 128)
-    f_keep, f_send = call(features_body, (f_shape, f_shape), "v")(features)
-    g_keep, g_send, mix = call(
-        functools.partial(grads_body, owned), (g_shape, g_shape, mix_shape), "vss"
-    )(out_grad, mix_seed.T, style_of)
+    f_keep, f_send = call(features_body, (f_shape, f_shape), "v", flops=2 * 10**9)(features)
+    g_keep, g_send = call(functools.partial(grads_body, owned), (g_shape, g_shape), "v")(out_grad)
+    mix = call(weights_body, mix_shape, "ssa")(mix_seed.T, style_of, g_send)
 
     f_yn = send(f_send, over_y)
     g_xn = send(g_send, over_x)

time: 49.7 us -> 48.5 us (0.976)
  local copies, waits for them, and re-layouts: 2.76 us -> 1.11 us
  starting transfers between devices: 24.7 us -> 26.2 us
  waiting for transfers between devices: 11.5 us -> 10.5 us
    unnamed x8, local copies, waits for them, and re-layouts: 2.76 us -> 1.11 us
    ppermute x15, starting transfers between devices: 24.7 us -> 26.2 us  [send(): return lax.ppermute(value, 'wide', pairs)]
    ppermute x15, waiting for transfers between devices: 11.5 us -> 10.5 us  [send(): return lax.ppermute(value, 'wide', pairs)]
where the time goes in v1:
time: 48.5 us; the launch traced here: 48.4 us
  starting transfers between devices  26.2 us (54%)
  waiting for transfers between devices  10.5 us (22%)
  Pallas kernels  5.82 us (12%)
  blocking collectives  3.84 us (8%)
  local copies, waits for them, and re-layouts  1.11 us (2%)
  between operations  0.76 us (2%)
    ppermute x15, starting transfers between devices, send(): return lax.ppermute(value, 'wide', pairs)  26.2 us
    ppermute x15, waiting for transfers between devices, send(): return lax.ppermute(value, 'wide', pairs)  10.5 us
    all_gather x1, blocking collectives, local(): every_sum = lax.all_gather(own_sums, 'narrow', axis=0, tiled=True)  2.02 us
    all_gather x1, blocking collectives, local(): every_mix = lax.all_gather(mix[None], 'narrow', axis=0, tiled=True)  1.82 us
    pallas_call x1, Pallas kernels, local(): call(far_body, (sums, left, left, right), 'v' * 6, flops=5 * pair)  1.45 us
    pallas_call x1, Pallas kernels, local(): call(near_body, (sums, lefts, lefts, rights), 'v' * 6, flops=5 * pair)  1.33 us
    unnamed x8, local copies, waits for them, and re-layouts  1.11 us
    pallas_call x1, Pallas kernels, local(): call(final_body, shape(*bank.shape), 'vvvv', ANY_SPEC, scratch=(pltpu.VME...  1.1 us
  transfers between devices with their start and end apart: 15, of which 6 were waited for; matrix products, arithmetic and copies ran while one was open for 0% of the time, Pallas kernels for 8%

profile of v1, /device:TPU:0, one launch (start us, length us, event | category | flops | bytes accessed | tf_op | source)
XLA Modules:
  0.0 48.4 jit_solution(17801028257405412580)
XLA Ops:
  0.0 1.1 %copy-done.3 = f32[1,1,512,256]{3,2,1,0:T(8,128)S(1)} copy-done((f32[1,1,512,256]{3,2,1,0:T(8,128)S(1)}, f32[1,1,512,256]{3,2,1,0:T(8,128)}, u32[]{:S(2)}) %copy-start.3) | copy-done | bytes 524312
  1.2 3.1 %collective-permute-start = (f32[512,128]{1,0:T(8,128)S(1)}, f32[512,128]{1,0:T(8,128)S(1)}, u32[]{:S(2)}, u32[]{:S(2)}) collective-permute-start(f32[512,128]{1,0:T(8,128)S(1)} %get-tuple-element.33), channel_id=1, source_target_pairs={{0,4},{2,6},{4,0},{6,2},{8,12},{10,14},{12,8},{14,10},{16,20},{18,... | collective-permute-start | bytes 786440 | tf_op jit(solution)/shard_map/ppermute | solution.py:215
  4.4 1.6 %collective-permute-start.5 = (f32[128,512]{1,0:T(8,128)S(1)}, f32[128,512]{1,0:T(8,128)S(1)}, u32[]{:S(2)}, u32[]{:S(2)}) collective-permute-start(f32[128,512]{1,0:T(8,128)S(1)} %get-tuple-element.29.after_ref), channel_id=1, source_target_pairs={{0,2},{2,0},{4,6},{6,4},{8,10},{10,8},{12,14},{14,12},{16,18},{18,... | collective-permute-start | bytes 786440 | tf_op jit(solution)/shard_map/ppermute | solution.py:215
  6.6 0.6 %shard_map.56 = f32[16,128]{1,0:T(8,128)S(1)} custom-call(s32[4,16]{1,0:T(4,128)S(1)} %bitcast.4, s32[1]{0:T(128)S(6)} %copy.10.style_ref, f32[128,512]{1,0:T(8,128)S(1)} %get-tuple-element.29.after_ref), custom_call_target="tpu_custom_call" | custom-call | bytes 1048576 | tf_op jit(solution)/shard_map/pallas_call | solution.py:237
  7.2 1.8 %all-gather = f32[32,128]{1,0:T(8,128)S(1)} all-gather(f32[16,128]{1,0:T(8,128)S(1)} %shard_map.56), channel_id=2, replica_groups=mesh['wide'=16,'narrow'=2] {'narrow'}, dimensions={0}, use_global_device_ids=true | all-gather | bytes 24576 | tf_op jit(solution)/shard_map/all_gather | solution.py:241
  9.9 0.6 %collective-permute-done.refs_2_ = f32[512,128]{1,0:T(8,128)S(1)} collective-permute-done((f32[512,128]{1,0:T(8,128)S(1)}, f32[512,128]{1,0:T(8,128)S(1)}, u32[]{:S(2)}, u32[]{:S(2)}) %collective-permute-start) | collective-permute-done | bytes 262176 | tf_op jit(solution)/shard_map/ppermute | solution.py:215
  10.6 3.9 %collective-permute-start.1 = (f32[512,128]{1,0:T(8,128)S(1)}, f32[512,128]{1,0:T(8,128)S(1)}, u32[]{:S(2)}, u32[]{:S(2)}) collective-permute-start(f32[512,128]{1,0:T(8,128)S(1)} %broadcast_select_fusion.1), channel_id=1, source_target_pairs={{0,24},{2,10},{4,28},{6,14},{8,0},{10,18},{12,4},{14,22},{16,8},{1... | collective-permute-start | bytes 786440 | tf_op jit(solution)/shard_map/ppermute | solution.py:215
  14.4 1.7 %collective-permute-start.6 = (f32[128,512]{1,0:T(8,128)S(1)}, f32[128,512]{1,0:T(8,128)S(1)}, u32[]{:S(2)}, u32[]{:S(2)}) collective-permute-start(f32[128,512]{1,0:T(8,128)S(1)} %collective-permute-done.5.refs_4_), channel_id=1, source_target_pairs={{0,4},{2,6},{4,0},{6,2},{8,12},{10,14},{12,8},{14,10},{16,20},{18,... | collective-permute-start | bytes 786440 | tf_op jit(solution)/shard_map/ppermute | solution.py:215
  16.1 2.4 %collective-permute-done.2.refs_5_ = f32[128,512]{1,0:T(8,128)S(1)} collective-permute-done((f32[128,512]{1,0:T(8,128)S(1)}, f32[128,512]{1,0:T(8,128)S(1)}, u32[]{:S(2)}, u32[]{:S(2)}) %collective-permute-start.2) | collective-permute-done | bytes 262176 | tf_op jit(solution)/shard_map/ppermute | solution.py:215
  18.5 3.7 %collective-permute-start.3 = (f32[128,512]{1,0:T(8,128)S(1)}, f32[128,512]{1,0:T(8,128)S(1)}, u32[]{:S(2)}, u32[]{:S(2)}) collective-permute-start(f32[128,512]{1,0:T(8,128)S(1)} %broadcast_select_fusion), channel_id=1, source_target_pairs={{0,24},{2,10},{4,28},{6,14},{8,0},{10,18},{12,4},{14,22},{16,8},{1... | collective-permute-start | bytes 786440 | tf_op jit(solution)/shard_map/ppermute | solution.py:215
  22.2 1.3 %shard_map.59 = (f32[3,384,128]{2,1,0:T(8,128)S(1)}, bf16[3,384,512]{2,1,0:T(8,128)(2,1)S(1)}, bf16[3,384,512]{2,1,0:T(8,128)(2,1)S(1)}, bf16[3,512,256]{2,1,0:T(8,128)(2,1)S(1)}) custom-call(f32[512,128]{1,0:T(8,128)S(1)} %get-tuple-element.32.refs_0_, f32[512,128]{1,0:T(8,128)S(1)} %collective-permute-done.7.refs_1_, ...), custom_call_target="tpu_custom_call" | custom-call | flops 754974720 | bytes 1048576 | tf_op jit(solution)/shard_map/pallas_call | solution.py:265
  23.5 1.4 %shard_map.60 = (f32[3,384,128]{2,1,0:T(8,128)S(1)}, bf16[384,512]{1,0:T(8,128)(2,1)S(1)}, bf16[384,512]{1,0:T(8,128)(2,1)S(1)}, bf16[512,256]{1,0:T(8,128)(2,1)S(1)}) custom-call(f32[512,128]{1,0:T(8,128)S(1)} %collective-permute-done.4.f, f32[128,512]{1,0:T(8,128)S(1)} %collective-permute-done.6.g, f32[3,384,128]{2,1,0:T(8,128)S(1)} %get-tuple-element.35.acc_in, ...), custom_call_target="tpu_custom_call" | custom-call | flops 754974720 | bytes 1048576 | tf_op jit(solution)/shard_map/pallas_call | solution.py:268
  25.0 1.4 %collective-permute-done.3.refs_1_ = f32[128,512]{1,0:T(8,128)S(1)} collective-permute-done((f32[128,512]{1,0:T(8,128)S(1)}, f32[128,512]{1,0:T(8,128)S(1)}, u32[]{:S(2)}, u32[]{:S(2)}) %collective-permute-start.3) | collective-permute-done | bytes 262176 | tf_op jit(solution)/shard_map/ppermute | solution.py:215
  26.4 0.9 %shard_map.61 = (f32[9,16,128]{2,1,0:T(8,128)S(1)}, f32[9,16,128]{2,1,0:T(8,128)S(1)}, f32[9,16,128]{2,1,0:T(8,128)S(1)}, f32[9,16,128]{2,1,0:T(8,128)S(1)}, f32...) custom-call(f32[512,128]{1,0:T(8,128)S(1)} %collective-permute-done.1, ...), custom_call_target="tpu_custom_call" | custom-call | flops 301989888 | bytes 1048576 | tf_op jit(solution)/shard_map/pallas_call | solution.py:272
  27.3 0.6 %collective-permute-start.8 = (f32[9,16,128]{2,1,0:T(8,128)S(1)}, f32[9,16,128]{2,1,0:T(8,128)S(1)}, u32[]{:S(2)}, u32[]{:S(2)}) collective-permute-start(f32[9,16,128]{2,1,0:T(8,128)S(1)} %get-tuple-element.44), channel_id=1, source_target_pairs={{0,4},{2,6},{4,0},{6,2},{8,12},{10,14},{12,8},{14,10},{16,20},{18,... | collective-permute-start | bytes 221192 | tf_op jit(solution)/shard_map/ppermute | solution.py:215
  27.8 1.2 %collective-permute-start.9 = (f32[9,16,128]{2,1,0:T(8,128)S(1)}, f32[9,16,128]{2,1,0:T(8,128)S(1)}, u32[]{:S(2)}, u32[]{:S(2)}) collective-permute-start(f32[9,16,128]{2,1,0:T(8,128)S(1)} %get-tuple-element.45), channel_id=1, source_target_pairs={{0,8},{2,10},{4,12},{6,14},{8,0},{10,2},{12,4},{14,6},{16,24},{18,... | collective-permute-start | bytes 221192 | tf_op jit(solution)/shard_map/ppermute | solution.py:215
  29.0 1.8 %collective-permute-start.10 = (f32[9,16,128]{2,1,0:T(8,128)S(1)}, f32[9,16,128]{2,1,0:T(8,128)S(1)}, u32[]{:S(2)}, u32[]{:S(2)}) collective-permute-start(f32[9,16,128]{2,1,0:T(8,128)S(1)} %get-tuple-element.46), channel_id=1, source_target_pairs={{0,12},{2,14},{4,8},{6,10},{8,4},{10,6},{12,0},{14,2},{16,28},{18,... | collective-permute-start | bytes 221192 | tf_op jit(solution)/shard_map/ppermute | solution.py:215
  30.8 2.9 %collective-permute-start.11 = (f32[9,16,128]{2,1,0:T(8,128)S(1)}, f32[9,16,128]{2,1,0:T(8,128)S(1)}, u32[]{:S(2)}, u32[]{:S(2)}) collective-permute-start(f32[9,16,128]{2,1,0:T(8,128)S(1)} %get-tuple-element.47), channel_id=1, source_target_pairs={{0,16},{2,18},{4,20},{6,22},{8,24},{10,26},{12,28},{14,30},{16,0},... | collective-permute-start | bytes 221192 | tf_op jit(solution)/shard_map/ppermute | solution.py:215
  33.7 4.3 %collective-permute-start.13 = (f32[9,16,128]{2,1,0:T(8,128)S(1)}, f32[9,16,128]{2,1,0:T(8,128)S(1)}, u32[]{:S(2)}, u32[]{:S(2)}) collective-permute-start(f32[9,16,128]{2,1,0:T(8,128)S(1)} %get-tuple-element.49), channel_id=1, source_target_pairs={{0,24},{2,26},{4,28},{6,30},{8,16},{10,18},{12,20},{14,22},{16,8},... | collective-permute-start | bytes 221192 | tf_op jit(solution)/shard_map/ppermute | solution.py:215
  38.1 1.0 %collective-permute-start.14 = (f32[9,16,128]{2,1,0:T(8,128)S(1)}, f32[9,16,128]{2,1,0:T(8,128)S(1)}, u32[]{:S(2)}, u32[]{:S(2)}) collective-permute-start(f32[9,16,128]{2,1,0:T(8,128)S(1)} %get-tuple-element.50), channel_id=1, source_target_pairs={{0,28},{2,30},{4,24},{6,26},{8,20},{10,22},{12,16},{14,18},{16,12}... | collective-permute-start | bytes 221192 | tf_op jit(solution)/shard_map/ppermute | solution.py:215
  39.2 4.0 %collective-permute-done.12.refs_5_ = f32[9,16,128]{2,1,0:T(8,128)S(1)} collective-permute-done((f32[9,16,128]{2,1,0:T(8,128)S(1)}, f32[9,16,128]{2,1,0:T(8,128)S(1)}, u32[]{:S(2)}, u32[]{:S(2)}) %collective-permute-start.12) | collective-permute-done | bytes 73760 | tf_op jit(solution)/shard_map/ppermute | solution.py:215
  43.2 2.0 %collective-permute-done.14.refs_7_ = f32[9,16,128]{2,1,0:T(8,128)S(1)} collective-permute-done((f32[9,16,128]{2,1,0:T(8,128)S(1)}, f32[9,16,128]{2,1,0:T(8,128)S(1)}, u32[]{:S(2)}, u32[]{:S(2)}) %collective-permute-start.14) | collective-permute-done | bytes 73760 | tf_op jit(solution)/shard_map/ppermute | solution.py:215
  45.3 2.0 %all_gather.7.sums_ref = f32[2,18,16,128]{3,2,1,0:T(8,128)S(1)} all-gather(f32[1,18,16,128]{3,2,1,0:T(8,128)S(1)} %shard_map.62), channel_id=1, replica_groups=mesh['wide'=16,'narrow'=2] {'narrow'}, dimensions={0}, use_global_device_ids=true | all-gather | bytes 442368 | tf_op jit(solution)/shard_map/all_gather | solution.py:286
  47.3 1.1 %shard_map.63 = f32[4,16,2304]{2,1,0:T(8,128)} custom-call(f32[2,18,16,128]{3,2,1,0:T(8,128)S(1)} %all_gather.7.sums_ref, f32[2,16,128]{2,1,0:T(8,128)S(1)} %bitcast.3, f32[2,16,2304]{2,1,0:T(8,128)S(1)} %get-tuple-element.51.mixed_ref, f32[2,16,128]{2,1,0:T(8,128)S(1)} %get-tuple-element.52.scale_ref), custom_call_target="tpu_custom_call" | custom-call | bytes 1048576 | tf_op jit(solution)/shard_map/pallas_call | solution.py:287
  (27 shorter events, 1.4 us)
Async XLA Ops:
  0.0 4.2 %copy-start.1 = (f32[1,1,512,256]{3,2,1,0:T(8,128)S(1)}, f32[1,1,512,256]{3,2,1,0:T(8,128)}, u32[]{:S(2)}) copy-start(f32[1,1,512,256]{3,2,1,0:T(8,128)} %g_ref.1) | copy-start | bytes 1572868
  0.0 6.6 %copy-start.2 = (s32[16,4]{0,1:T(4,128)S(1)}, s32[16,4]{0,1:T(4,128)}, u32[]{:S(2)}) copy-start(s32[16,4]{0,1:T(4,128)} %param.8) | copy-start | bytes 772
  0.0 1.1 %copy-start.3 = (f32[1,1,512,256]{3,2,1,0:T(8,128)S(1)}, f32[1,1,512,256]{3,2,1,0:T(8,128)}, u32[]{:S(2)}) copy-start(f32[1,1,512,256]{3,2,1,0:T(8,128)} %f_ref.1) | copy-start | bytes 1572868
  1.1 7.9 %copy-start = (f32[4,16,2304]{2,1,0:T(8,128)S(1)}, f32[4,16,2304]{2,1,0:T(8,128)}, u32[]{:S(2)}) copy-start(f32[4,16,2304]{2,1,0:T(8,128)} %bank_ref.1) | copy-start | bytes 1769476
  1.2 9.4 %collective-permute-start = (f32[512,128]{1,0:T(8,128)S(1)}, f32[512,128]{1,0:T(8,128)S(1)}, u32[]{:S(2)}, u32[]{:S(2)}) collective-permute-start(f32[512,128]{1,0:T(8,128)S(1)} %get-tuple-element.33), channel_id=1, source_target_pairs={{0,4},{2,6},{4,0},{6,2},{8,12},{10,14},{12,8},{14,10},{16,20},{18,... | collective-permute-start | bytes 786440 | tf_op jit(solution)/shard_map/ppermute | solution.py:215
  4.4 10.0 %collective-permute-start.5 = (f32[128,512]{1,0:T(8,128)S(1)}, f32[128,512]{1,0:T(8,128)S(1)}, u32[]{:S(2)}, u32[]{:S(2)}) collective-permute-start(f32[128,512]{1,0:T(8,128)S(1)} %get-tuple-element.29.after_ref), channel_id=1, source_target_pairs={{0,2},{2,0},{4,6},{6,4},{8,10},{10,8},{12,14},{14,12},{16,18},{18,... | collective-permute-start | bytes 786440 | tf_op jit(solution)/shard_map/ppermute | solution.py:215
  9.3 9.2 %collective-permute-start.2 = (f32[128,512]{1,0:T(8,128)S(1)}, f32[128,512]{1,0:T(8,128)S(1)}, u32[]{:S(2)}, u32[]{:S(2)}) collective-permute-start(f32[128,512]{1,0:T(8,128)S(1)} %get-tuple-element.34.refs_3_), channel_id=1, source_target_pairs={{0,4},{2,6},{4,0},{6,2},{8,12},{10,14},{12,8},{14,10},{16,20},{18,... | collective-permute-start | bytes 786440 | tf_op jit(solution)/shard_map/ppermute | solution.py:215
  9.8 12.4 %collective-permute-start.7 = (f32[512,128]{1,0:T(8,128)S(1)}, f32[512,128]{1,0:T(8,128)S(1)}, u32[]{:S(2)}, u32[]{:S(2)}) collective-permute-start(f32[512,128]{1,0:T(8,128)S(1)} %get-tuple-element.32.refs_0_), channel_id=1, source_target_pairs={{0,2},{2,0},{4,6},{6,4},{8,10},{10,8},{12,14},{14,12},{16,18},{18,... | collective-permute-start | bytes 786440 | tf_op jit(solution)/shard_map/ppermute | solution.py:215
  10.6 14.4 %collective-permute-start.1 = (f32[512,128]{1,0:T(8,128)S(1)}, f32[512,128]{1,0:T(8,128)S(1)}, u32[]{:S(2)}, u32[]{:S(2)}) collective-permute-start(f32[512,128]{1,0:T(8,128)S(1)} %broadcast_select_fusion.1), channel_id=1, source_target_pairs={{0,24},{2,10},{4,28},{6,14},{8,0},{10,18},{12,4},{14,22},{16,8},{1... | collective-permute-start | bytes 786440 | tf_op jit(solution)/shard_map/ppermute | solution.py:215
  14.4 9.1 %collective-permute-start.4 = (f32[512,128]{1,0:T(8,128)S(1)}, f32[512,128]{1,0:T(8,128)S(1)}, u32[]{:S(2)}, u32[]{:S(2)}) collective-permute-start(f32[512,128]{1,0:T(8,128)S(1)} %collective-permute-done.refs_2_), channel_id=1, source_target_pairs={{0,2},{2,0},{4,6},{6,4},{8,10},{10,8},{12,14},{14,12},{16,18},{18,... | collective-permute-start | bytes 786440 | tf_op jit(solution)/shard_map/ppermute | solution.py:215
  14.4 9.1 %collective-permute-start.6 = (f32[128,512]{1,0:T(8,128)S(1)}, f32[128,512]{1,0:T(8,128)S(1)}, u32[]{:S(2)}, u32[]{:S(2)}) collective-permute-start(f32[128,512]{1,0:T(8,128)S(1)} %collective-permute-done.5.refs_4_), channel_id=1, source_target_pairs={{0,4},{2,6},{4,0},{6,2},{8,12},{10,14},{12,8},{14,10},{16,20},{18,... | collective-permute-start | bytes 786440 | tf_op jit(solution)/shard_map/ppermute | solution.py:215
  18.5 7.9 %collective-permute-start.3 = (f32[128,512]{1,0:T(8,128)S(1)}, f32[128,512]{1,0:T(8,128)S(1)}, u32[]{:S(2)}, u32[]{:S(2)}) collective-permute-start(f32[128,512]{1,0:T(8,128)S(1)} %broadcast_select_fusion), channel_id=1, source_target_pairs={{0,24},{2,10},{4,28},{6,14},{8,0},{10,18},{12,4},{14,22},{16,8},{1... | collective-permute-start | bytes 786440 | tf_op jit(solution)/shard_map/ppermute | solution.py:215
  27.3 6.4 %collective-permute-start.8 = (f32[9,16,128]{2,1,0:T(8,128)S(1)}, f32[9,16,128]{2,1,0:T(8,128)S(1)}, u32[]{:S(2)}, u32[]{:S(2)}) collective-permute-start(f32[9,16,128]{2,1,0:T(8,128)S(1)} %get-tuple-element.44), channel_id=1, source_target_pairs={{0,4},{2,6},{4,0},{6,2},{8,12},{10,14},{12,8},{14,10},{16,20},{18,... | collective-permute-start | bytes 221192 | tf_op jit(solution)/shard_map/ppermute | solution.py:215
  27.8 10.2 %collective-permute-start.9 = (f32[9,16,128]{2,1,0:T(8,128)S(1)}, f32[9,16,128]{2,1,0:T(8,128)S(1)}, u32[]{:S(2)}, u32[]{:S(2)}) collective-permute-start(f32[9,16,128]{2,1,0:T(8,128)S(1)} %get-tuple-element.45), channel_id=1, source_target_pairs={{0,8},{2,10},{4,12},{6,14},{8,0},{10,2},{12,4},{14,6},{16,24},{18,... | collective-permute-start | bytes 221192 | tf_op jit(solution)/shard_map/ppermute | solution.py:215
  29.0 10.0 %collective-permute-start.10 = (f32[9,16,128]{2,1,0:T(8,128)S(1)}, f32[9,16,128]{2,1,0:T(8,128)S(1)}, u32[]{:S(2)}, u32[]{:S(2)}) collective-permute-start(f32[9,16,128]{2,1,0:T(8,128)S(1)} %get-tuple-element.46), channel_id=1, source_target_pairs={{0,12},{2,14},{4,8},{6,10},{8,4},{10,6},{12,0},{14,2},{16,28},{18,... | collective-permute-start | bytes 221192 | tf_op jit(solution)/shard_map/ppermute | solution.py:215
  30.8 8.4 %collective-permute-start.11 = (f32[9,16,128]{2,1,0:T(8,128)S(1)}, f32[9,16,128]{2,1,0:T(8,128)S(1)}, u32[]{:S(2)}, u32[]{:S(2)}) collective-permute-start(f32[9,16,128]{2,1,0:T(8,128)S(1)} %get-tuple-element.47), channel_id=1, source_target_pairs={{0,16},{2,18},{4,20},{6,22},{8,24},{10,26},{12,28},{14,30},{16,0},... | collective-permute-start | bytes 221192 | tf_op jit(solution)/shard_map/ppermute | solution.py:215
  33.7 9.5 %collective-permute-start.12 = (f32[9,16,128]{2,1,0:T(8,128)S(1)}, f32[9,16,128]{2,1,0:T(8,128)S(1)}, u32[]{:S(2)}, u32[]{:S(2)}) collective-permute-start(f32[9,16,128]{2,1,0:T(8,128)S(1)} %get-tuple-element.48), channel_id=1, source_target_pairs={{0,20},{2,22},{4,16},{6,18},{8,28},{10,30},{12,24},{14,26},{16,4},... | collective-permute-start | bytes 221192 | tf_op jit(solution)/shard_map/ppermute | solution.py:215
  33.7 9.5 %collective-permute-start.13 = (f32[9,16,128]{2,1,0:T(8,128)S(1)}, f32[9,16,128]{2,1,0:T(8,128)S(1)}, u32[]{:S(2)}, u32[]{:S(2)}) collective-permute-start(f32[9,16,128]{2,1,0:T(8,128)S(1)} %get-tuple-element.49), channel_id=1, source_target_pairs={{0,24},{2,26},{4,28},{6,30},{8,16},{10,18},{12,20},{14,22},{16,8},... | collective-permute-start | bytes 221192 | tf_op jit(solution)/shard_map/ppermute | solution.py:215
  38.1 7.2 %collective-permute-start.14 = (f32[9,16,128]{2,1,0:T(8,128)S(1)}, f32[9,16,128]{2,1,0:T(8,128)S(1)}, u32[]{:S(2)}, u32[]{:S(2)}) collective-permute-start(f32[9,16,128]{2,1,0:T(8,128)S(1)} %get-tuple-element.50), channel_id=1, source_target_pairs={{0,28},{2,30},{4,24},{6,26},{8,20},{10,22},{12,16},{14,18},{16,12}... | collective-permute-start | bytes 221192 | tf_op jit(solution)/shard_map/ppermute | solution.py:215

commit v2 on v1

--- a/solution.py
+++ b/solution.py
@@ -92,96 +92,132 @@
     )
 
 
-def operands(f, g, lh, ll, rt):
+def left(g, high, low):
+    high[...], low[...] = shifted(g[...])
+
+
+def right(f, out):
     half = f.shape[1]
-    lh[...], ll[...] = shifted(g[...])
     high, low = split(f[...])
-    rt[:, :half] = high
-    rt[:, half:] = low
-
-
-def near_body(*refs):
-    fs, gs, acc, lh, ll, rt = refs[0:3], refs[3:6], *refs[6:]
-    _, _, x, _ = place()
-    half = fs[0].shape[1]
-    for role in range(3):
-        operands(fs[role], gs[role], lh.at[role], ll.at[role], rt.at[role])
-
-    def mul(a, b):
-        return product(lh[a], ll[a], rt[b], half)
-
-    up = jnp.where(x == 0, 2, 0)
-    acc[1] = mul(0, 0) + mul(1, 1) + mul(2, 2)
-    acc[up] = mul(0, 1)
-    acc[2 - up] = mul(1, 0)
-
-
-def far_body(f, g, acc_in, lh, ll, rt, acc, lh_far, ll_far, rt_far):
+    out[:, :half] = high
+    out[:, half:] = low
+
+
+def mul(lefts, role, rights, other):
+    half = rights.shape[2] // 2
+    return product(lefts[0][role], lefts[1][role], rights[other], half)
+
+
+def first_body(f_own, f_yn, g_own, g_xn, mid, side, lh, ll, rt):
     _, _, x, y = place()
-    half = f.shape[1]
-    operands(f, g, lh_far, ll_far, rt_far)
-    far = (lh_far, ll_far, rt_far)
-    own, xn, yn = [(lh.at[i], ll.at[i], rt.at[i]) for i in range(3)]
-
-    def mul(a, b):
-        return product(a[0][...], a[1][...], b[2][...], half)
-
-    up = jnp.where(x == 0, 2, 0)
-    acc[1] = acc_in[1] + mul(far, far)
-    acc[up] = acc_in[up] + mul(yn, far)
-    acc[2 - up] = acc_in[2 - up] + mul(far, yn)
-    onward = jnp.where(y == 0, 2, 0)
-
-    def middle(a, b):
-        acc[onward] += mul(a, b)
-        acc[2 - onward] += mul(b, a)
-
-    pl.when(x == y)(lambda: middle(xn, yn))
-    pl.when(x != y)(lambda: middle(own, far))
-
-
-def edge_body(groups, owned, *refs):
-    fe, ge, acc_in, lh, ll, rt, lh_far, ll_far, rt_far = refs[:9]
-    outs, acc, lh_ex, ll_ex, rt_ex = refs[9:-4], *refs[-4:]
+    left(g_own, lh.at[0], ll.at[0])
+    left(g_xn, lh.at[1], ll.at[1])
+    right(f_own, rt.at[0])
+    right(f_yn, rt.at[1])
+    lefts = (lh, ll)
+    mid[...] = mul(lefts, 0, rt, 0)
+    side[x] = mul(lefts, 1, rt, 0)
+    side[1 - x] = jnp.zeros(side.shape[1:], F32)
+
+    @pl.when(x == y)
+    def _():
+        side[1 - y] += mul(lefts, 1, rt, 1)
+
+
+def near_body(groups, f_xn, g_yn, f_even, f_odd, mid_in, side_in, lh, ll, rt, mid, side, lh_yn, ll_yn, rt_more):
     group, _, x, y = place()
-    half = fe.shape[1]
-    operands(fe, ge, lh_ex, ll_ex, rt_ex)
+    left(g_yn, lh_yn.at[0], ll_yn.at[0])
+    right(f_xn, rt_more.at[0])
+    from_even = group % 2 == x
+    pl.when(from_even)(lambda: right(f_even, rt_more.at[1]))
+    pl.when(~from_even)(lambda: right(f_odd, rt_more.at[1]))
 
     @pl.when(group == jnp.where(x == 1, 0, groups - 1))
     def _():
-        lh_ex[...] = jnp.zeros_like(lh_ex)
-        ll_ex[...] = jnp.zeros_like(ll_ex)
-        rt_ex[...] = jnp.zeros_like(rt_ex)
-
-    up = jnp.where(x == 0, 2, 0)
-    acc[1] = acc_in[1]
-
-    def outer(lh_in, ll_in, rt_in):
-        acc[up] = acc_in[up] + product(lh_in[...], ll_in[...], rt_ex[...], half)
-        acc[2 - up] = acc_in[2 - up] + product(lh_ex[...], ll_ex[...], rt_in[...], half)
-
-    pl.when(x == y)(lambda: outer(lh_far, ll_far, rt_far))
-    pl.when(x != y)(lambda: outer(lh.at[1], ll.at[1], rt.at[1]))
-    n_out = ge.shape[0]
+        rt_more[1] = jnp.zeros(rt_more.shape[1:], BF16)
+
+    lefts, lefts_yn = (lh, ll), (lh_yn, ll_yn)
+    mid[...] = mid_in[...] + mul(lefts, 1, rt_more, 0) + mul(lefts_yn, 0, rt, 1)
+    side[x] = side_in[x]
+    side[1 - x] = side_in[1 - x] + mul(lefts, 0, rt_more, 0)
+
+    @pl.when(x == y)
+    def _():
+        side[y] += mul(lefts_yn, 0, rt_more, 0)
+
+    @pl.when(x != y)
+    def _():
+        side[1 - x] += mul(lefts, 1, rt_more, 1)
+
+
+def far_body(f_dg, g_dg, mid_in, side_in, lh, ll, rt, lh_yn, ll_yn, rt_more, mid, side, rt_far, lh_far, ll_far):
+    _, _, x, y = place()
+    left(g_dg, lh_far.at[0], ll_far.at[0])
+    right(f_dg, rt_far.at[0])
+    lefts, lefts_yn, lefts_far = (lh, ll), (lh_yn, ll_yn), (lh_far, ll_far)
+    mid[...] = mid_in[...] + mul(lefts_far, 0, rt_far, 0)
+    side[x] = side_in[x] + mul(lefts_far, 0, rt, 1)
+    side[1 - x] = side_in[1 - x] + mul(lefts_yn, 0, rt_far, 0)
+
+    @pl.when(x == y)
+    def _():
+        side[1 - x] += mul(lefts_far, 0, rt_more, 1)
+
+    @pl.when(x != y)
+    def _():
+        side[1 - y] += mul(lefts, 0, rt_far, 0)
+        side[y] += mul(lefts_far, 0, rt, 0)
+
+
+def edge_body(groups, owned, g_even, g_odd, mid, side_in, rt_more, rt_far, *refs):
+    outs, odds, evens, side, lh, ll = refs[:-5], *refs[-5:]
+    group, _, x, y = place()
+    n_out = g_even.shape[0]
+    from_even = group % 2 == x
+    pl.when(from_even)(lambda: left(g_even, lh.at[0], ll.at[0]))
+    pl.when(~from_even)(lambda: left(g_odd, lh.at[0], ll.at[0]))
+
+    @pl.when(group == jnp.where(x == 1, 0, groups - 1))
+    def _():
+        lh[...] = jnp.zeros_like(lh)
+        ll[...] = jnp.zeros_like(ll)
+
+    side[1 - x] = side_in[1 - x]
+
+    @pl.when(x == y)
+    def _():
+        side[x] = side_in[x] + mul((lh, ll), 0, rt_far, 0)
+
+    @pl.when(x != y)
+    def _():
+        side[x] = side_in[x] + mul((lh, ll), 0, rt_more, 0)
+
     rows = 2 * owned
     for m in range(groups):
         start = pl.multiple_of((group ^ m) * rows, rows)
-        for a in range(3):
+        across = (odds if m % 2 else evens).at[m // 2]
+        for a, sums in enumerate((side.at[0], mid, side.at[1])):
             for b in range(3):
-                both = acc[a, pl.ds(b * n_out + start, rows), :]
+                both = sums[pl.ds(b * n_out + start, rows), :]
                 low, high = both[:owned], both[owned:]
-                outs[2 * m][3 * a + b] = jnp.where(y == 0, low, high)
-                outs[2 * m + 1][3 * a + b] = jnp.where(y == 0, high, low)
-
-
-def sum_body(*refs):
+                outs[m][3 * a + b] = jnp.where(y == 0, low, high)
+                across[3 * a + b] = jnp.where(y == 0, high, low)
+
+
+def pair_body(*refs):
+    mine, theirs, outs = refs[0], refs[1], refs[2:]
+    for k, out in enumerate(outs):
+        out[...] = mine[k] + theirs[k]
+
+
+def sum_body(groups, *refs):
     parts, out = refs[:-1], refs[-1]
     taps = parts[0].shape[0]
-    for d in range(2):
+    for d, terms in enumerate((parts[:groups], parts[groups:])):
         for t in range(taps):
-            total = parts[d][t]
-            for part in parts[d + 2 :: 2]:
-                total = total + part[t]
+            total = terms[0][t]
+            for term in terms[1:]:
+                total = total + term[t]
             out[0, d * taps + t] = total
 
 
@@ -211,8 +247,8 @@
         copy.wait()
 
 
-def send(value, pairs):
-    return lax.ppermute(value, "wide", pairs)
+def send(value, pairs, axes="wide"):
+    return lax.ppermute(value, axes, pairs)
 
 
 def local(features, out_grad, bank, mix_seed, style_of):
@@ -225,7 +261,16 @@
     everyone = range(size)
     over_x = [(i, i ^ 1) for i in everyone]
     over_y = [(i, i ^ 2) for i in everyone]
-    outward = [(i, (i + 4 if i % 2 else i - 4) % size) for i in everyone]
+    cores = lax.axis_size("narrow")
+    even = [(i, i ^ 4) for i in everyone]
+    odd = []
+    for i in everyone:
+        group, member = i // 4, i % 4
+        other = (group - 1 ^ 1) + 1
+        for c in range(cores):
+            at_edge = other in (0, groups + 1) or not 0 <= other < groups
+            to = (i, c ^ 1) if at_edge else (4 * other + member, c)
+            odd.append((i * cores + c, to[0] * cores + to[1]))
 
     def shape(*dims, dtype=F32):
         return jax.ShapeDtypeStruct(dims, dtype)
@@ -253,36 +298,64 @@
     g_dg = send(g_xn, over_y)
     me = lax.axis_index("wide")
     same = (me % 2) == ((me // 2) % 2)
-    f_ex = send(jnp.where(same, f_keep, f_yn), outward)
-    g_ex = send(jnp.where(same, g_keep, g_yn), outward)
+    f_out = jnp.where(same, f_keep, f_yn)
+    g_out = jnp.where(same, g_keep, g_yn)
+    both = ("wide", "narrow")
+    f_even = send(f_out, even)
+    f_odd = send(f_out, odd, both)
+    g_even = send(g_out, even)
+    g_odd = send(g_out, odd, both)
 
     pair = 2 * 3 * 3 * half_out * half_in * map_width
-    sums = shape(3, 3 * half_out, half_in)
-    left = shape(3 * half_out, map_width, dtype=BF16)
-    right = shape(map_width, 2 * half_in, dtype=BF16)
-    lefts = shape(3, *left.shape, dtype=BF16)
-    rights = shape(3, *right.shape, dtype=BF16)
-    acc, *near = call(near_body, (sums, lefts, lefts, rights), "v" * 6, flops=5 * pair)(
-        f_keep, f_xn, f_yn, g_keep, g_xn, g_yn
-    )
-    acc, *far = call(far_body, (sums, left, left, right), "v" * 6, flops=5 * pair)(
-        f_dg, g_dg, acc, *near
-    )
+    mids = shape(3 * half_out, half_in)
+    sides = shape(2, *mids.shape)
+
+    def lefts(count):
+        return shape(count, 3 * half_out, map_width, dtype=BF16)
+
+    def rights(count):
+        return shape(count, map_width, 2 * half_in, dtype=BF16)
+
+    mid, side, lh, ll, rt = call(
+        first_body, (mids, sides, lefts(2), lefts(2), rights(2)), "vvvv", flops=3 * pair
+    )(f_keep, f_yn, g_keep, g_xn)
+    mid, side, *more = call(
+        functools.partial(near_body, groups),
+        (mids, sides, lefts(1), lefts(1), rights(2)),
+        "v" * 9,
+        flops=4 * pair,
+    )(f_xn, g_yn, f_even, f_odd, mid, side, lh, ll, rt)
+    mid, side, rt_far = call(
+        far_body,
+        (mids, sides, rights(1)),
+        "v" * 10,
+        flops=5 * pair,
+        scratch=[pltpu.VMEM(lefts(1).shape, BF16)] * 2,
+    )(f_dg, g_dg, mid, side, lh, ll, rt, *more)
     piece = shape(9, owned, half_in)
-    blocks = call(
+    stack = shape(groups // 2, *piece.shape)
+    *blocks, odds, evens = call(
         functools.partial(edge_body, groups, owned),
-        [piece] * (2 * groups),
-        "v" * 9,
-        flops=2 * pair,
-        scratch=[pltpu.VMEM(a.shape, a.dtype) for a in (sums, left, left, right)],
-    )(f_ex, g_ex, acc, *near, *far)
-    parts = [blocks[0]] + [
-        send(blocks[n], [(i, i ^ (2 * n)) for i in everyone])
-        for n in range(1, 2 * groups)
-    ]
-    own_sums = call(sum_body, shape(1, 18, owned, half_in), "v" * (2 * groups))(
-        *parts
-    )
+        [piece] * groups + [stack] * 2,
+        "v" * 6,
+        flops=pair,
+        scratch=[
+            pltpu.VMEM(sides.shape, F32),
+            pltpu.VMEM(lefts(1).shape, BF16),
+            pltpu.VMEM(lefts(1).shape, BF16),
+        ],
+    )(g_even, g_odd, mid, side, more[2], rt_far)
+
+    def hop(m, d):
+        return [(i, i ^ (4 * m + 2 * d)) for i in everyone]
+
+    theirs = send(odds, hop(1, 0))
+    parts = [blocks[0]] + [send(blocks[m], hop(m, 0)) for m in range(1, groups)]
+    pairs = call(pair_body, [piece] * (groups // 2), "vv")(evens, theirs)
+    parts += [send(pairs[k], hop(2 * k, 1)) for k in range(groups // 2)]
+    own_sums = call(
+        functools.partial(sum_body, groups), shape(1, 18, owned, half_in), "v" * len(parts)
+    )(*parts)
     every_sum = lax.all_gather(own_sums, "narrow", axis=0, tiled=True)
     return call(
         final_body,

time: 48.5 us -> 44.6 us (0.920)
  starting transfers between devices: 26.2 us -> 22.7 us
  waiting for transfers between devices: 10.5 us -> 9.03 us
  Pallas kernels: 5.82 us -> 6.68 us
    ppermute x15 -> x16, starting transfers between devices: 26.2 us -> 22.7 us  [send(): return lax.ppermute(value, axes, pairs)]
    ppermute x15 -> x16, waiting for transfers between devices: 10.5 us -> 9.03 us  [send(): return lax.ppermute(value, axes, pairs)]
    pallas_call x4 -> x6, Pallas kernels: 3.7 us -> 4.56 us  [the longest x1 1.47 us: local(): call(functools.partial(near_body, groups), (mids, sides, lefts(1), lefts(...]
  transfers between devices with their start and end apart: 15 -> 16, of which waited for: 6 -> 7; matrix products, arithmetic and copies ran while one was open for 0% -> 0% of each run, Pallas kernels for 8% -> 11%
where the time goes in v2:
time: 44.6 us; the launch traced here: 44.2 us
  starting transfers between devices  22.7 us (51%)
  waiting for transfers between devices  9.03 us (20%)
  Pallas kernels  6.68 us (15%)
  blocking collectives  3.84 us (9%)
  local copies, waits for them, and re-layouts  1.11 us (2%)
  between operations  0.77 us (2%)
    ppermute x16, starting transfers between devices, send(): return lax.ppermute(value, axes, pairs)  22.7 us
    ppermute x16, waiting for transfers between devices, send(): return lax.ppermute(value, axes, pairs)  9.03 us
    all_gather x1, blocking collectives, local(): every_sum = lax.all_gather(own_sums, 'narrow', axis=0, tiled=True)  2.02 us
    all_gather x1, blocking collectives, local(): every_mix = lax.all_gather(mix[None], 'narrow', axis=0, tiled=True)  1.82 us
    pallas_call x1, Pallas kernels, local(): call(functools.partial(near_body, groups), (mids, sides, lefts(1), lefts(...  1.47 us
    pallas_call x1, Pallas kernels, local(): call(far_body, (mids, sides, rights(1)), 'v' * 10, flops=5 * pair, scratc...  1.26 us
    pallas_call x1, Pallas kernels, local(): call(first_body, (mids, sides, lefts(2), lefts(2), rights(2)), 'vvvv', fl...  1.11 us
    unnamed x8, local copies, waits for them, and re-layouts  1.11 us
  transfers between devices with their start and end apart: 16, of which 7 were waited for; matrix products, arithmetic and copies ran while one was open for 0% of the time, Pallas kernels for 11%

profile of v2, /device:TPU:0, one launch (start us, length us, event | category | flops | bytes accessed | tf_op | source)
XLA Modules:
  0.0 44.2 jit_solution(5315295797090170228)
XLA Ops:
  0.0 1.1 %copy-done.3 = f32[1,1,512,256]{3,2,1,0:T(8,128)S(1)} copy-done((f32[1,1,512,256]{3,2,1,0:T(8,128)S(1)}, f32[1,1,512,256]{3,2,1,0:T(8,128)}, u32[]{:S(2)}) %copy-start.3) | copy-done | bytes 524312
  1.2 3.1 %collective-permute-start.3 = (f32[512,128]{1,0:T(8,128)S(1)}, f32[512,128]{1,0:T(8,128)S(1)}, u32[]{:S(2)}, u32[]{:S(2)}) collective-permute-start(f32[512,128]{1,0:T(8,128)S(1)} %get-tuple-element.38), channel_id=1, source_target_pairs={{0,4},{2,6},{4,0},{6,2},{8,12},{10,14},{12,8},{14,10},{16,20},{18,... | collective-permute-start | bytes 786440 | tf_op jit(solution)/shard_map/ppermute | solution.py:251
  4.4 1.6 %collective-permute-start.5 = (f32[128,512]{1,0:T(8,128)S(1)}, f32[128,512]{1,0:T(8,128)S(1)}, u32[]{:S(2)}, u32[]{:S(2)}) collective-permute-start(f32[128,512]{1,0:T(8,128)S(1)} %get-tuple-element.34.after_ref), channel_id=1, source_target_pairs={{0,2},{2,0},{4,6},{6,4},{8,10},{10,8},{12,14},{14,12},{16,18},{18,... | collective-permute-start | bytes 786440 | tf_op jit(solution)/shard_map/ppermute | solution.py:251
  7.2 1.8 %all-gather = f32[32,128]{1,0:T(8,128)S(1)} all-gather(f32[16,128]{1,0:T(8,128)S(1)} %shard_map.56), channel_id=2, replica_groups=mesh['wide'=16,'narrow'=2] {'narrow'}, dimensions={0}, use_global_device_ids=true | all-gather | bytes 24576 | tf_op jit(solution)/shard_map/all_gather | solution.py:286
  9.9 0.6 %collective-permute-done.3.f_yn = f32[512,128]{1,0:T(8,128)S(1)} collective-permute-done((f32[512,128]{1,0:T(8,128)S(1)}, f32[512,128]{1,0:T(8,128)S(1)}, u32[]{:S(2)}, u32[]{:S(2)}) %collective-permute-start.3) | collective-permute-done | bytes 262176 | tf_op jit(solution)/shard_map/ppermute | solution.py:251
  10.6 1.9 %collective-permute-start.8 = (f32[512,128]{1,0:T(8,128)S(1)}, f32[512,128]{1,0:T(8,128)S(1)}, u32[]{:S(2)}, u32[]{:S(2)}) collective-permute-start(f32[512,128]{1,0:T(8,128)S(1)} %broadcast_select_fusion), channel_id=1, source_target_pairs={{0,8},{2,10},{4,12},{6,14},{8,0},{10,2},{12,4},{14,6},{16,24},{18,... | collective-permute-start | bytes 786440 | tf_op jit(solution)/shard_map/ppermute | solution.py:251
  12.4 2.4 %collective-permute-start.4 = (f32[512,128]{1,0:T(8,128)S(1)}, f32[512,128]{1,0:T(8,128)S(1)}, u32[]{:S(2)}, u32[]{:S(2)}) collective-permute-start(f32[512,128]{1,0:T(8,128)S(1)} %collective-permute-done.3.f_yn), channel_id=1, source_target_pairs={{0,2},{2,0},{4,6},{6,4},{8,10},{10,8},{12,14},{14,12},{16,18},{18,... | collective-permute-start | bytes 786440 | tf_op jit(solution)/shard_map/ppermute | solution.py:251
  14.8 2.8 %collective-permute-done.g_yn = f32[128,512]{1,0:T(8,128)S(1)} collective-permute-done((f32[128,512]{1,0:T(8,128)S(1)}, f32[128,512]{1,0:T(8,128)S(1)}, u32[]{:S(2)}, u32[]{:S(2)}) %collective-permute-start) | collective-permute-done | bytes 262176 | tf_op jit(solution)/shard_map/ppermute | solution.py:251
  18.2 0.8 %collective-permute-done.7.f_xn = f32[512,128]{1,0:T(8,128)S(1)} collective-permute-done((f32[512,128]{1,0:T(8,128)S(1)}, f32[512,128]{1,0:T(8,128)S(1)}, u32[]{:S(2)}, u32[]{:S(2)}) %collective-permute-start.7) | collective-permute-done | bytes 262176 | tf_op jit(solution)/shard_map/ppermute | solution.py:251
  19.0 1.6 %collective-permute-start.1 = (f32[128,512]{1,0:T(8,128)S(1)}, f32[128,512]{1,0:T(8,128)S(1)}, u32[]{:S(2)}, u32[]{:S(2)}) collective-permute-start(f32[128,512]{1,0:T(8,128)S(1)} %broadcast_select_fusion.1), channel_id=1, source_target_pairs={{0,8},{2,10},{4,12},{6,14},{8,0},{10,2},{12,4},{14,6},{16,24},{18,... | collective-permute-start | bytes 786440 | tf_op jit(solution)/shard_map/ppermute | solution.py:251
  20.6 1.1 %shard_map.59 = (f32[384,128]{1,0:T(8,128)S(1)}, f32[2,384,128]{2,1,0:T(8,128)S(1)}, bf16[2,384,512]{2,1,0:T(8,128)(2,1)S(1)}, bf16[2,384,512]{2,1,0:T(8,128)(2,1)S(1)}, bf16[2,512,256]{2,1,0:T(8,128)(2,1)S(1)}) custom-call(f32[512,128]{1,0:T(8,128)S(1)} %get-tuple-element.39.f_own, f32[512,128]{1,0:T(8,128)S(1)} %collective-permute-done.3.f_yn, ...), custom_call_target="tpu_custom_call" | custom-call | flops 452984832 | bytes 1048576 | tf_op jit(solution)/shard_map/pallas_call | solution.py:319
  21.7 1.5 %shard_map.60 = (f32[384,128]{1,0:T(8,128)S(1)}, f32[2,384,128]{2,1,0:T(8,128)S(1)}, bf16[1,384,512]{2,1,0:T(8,128)(2,1)S(1)}, bf16[1,384,512]{2,1,0:T(8,128)(2,1)S(1)}, bf16[2,512,256]{2,1,0:T(8,128)(2,1)S(1)}) custom-call(f32[512,128]{1,0:T(8,128)S(1)} %collective-permute-done.7.f_xn, f32[128,512]{1,0:T(8,128)S(1)} %collective-permute-done.g_yn, ...), custom_call_target="tpu_custom_call" | custom-call | flops 603979776 | bytes 1048576 | tf_op jit(solution)/shard_map/pallas_call | solution.py:322
  23.5 1.7 %collective-permute-done.6.g_dg = f32[128,512]{1,0:T(8,128)S(1)} collective-permute-done((f32[128,512]{1,0:T(8,128)S(1)}, f32[128,512]{1,0:T(8,128)S(1)}, u32[]{:S(2)}, u32[]{:S(2)}) %collective-permute-start.6) | collective-permute-done | bytes 262176 | tf_op jit(solution)/shard_map/ppermute | solution.py:251
  25.2 1.3 %shard_map.61 = (f32[384,128]{1,0:T(8,128)S(1)}, f32[2,384,128]{2,1,0:T(8,128)S(1)}, bf16[1,512,256]{2,1,0:T(8,128)(2,1)S(1)}) custom-call(f32[512,128]{1,0:T(8,128)S(1)} %collective-permute-done.4.f_dg, f32[128,512]{1,0:T(8,128)S(1)} %collective-permute-done.6.g_dg, f32[384,128]{1,0:T(8,128)S(1)} %get-tuple-element.45.mid_in, ...), custom_call_target="tpu_custom_call" | custom-call | flops 754974720 | bytes 1048576 | tf_op jit(solution)/shard_map/pallas_call | solution.py:328
  26.5 0.7 %shard_map.62 = (f32[9,16,128]{2,1,0:T(8,128)S(1)}, f32[9,16,128]{2,1,0:T(8,128)S(1)}, f32[9,16,128]{2,1,0:T(8,128)S(1)}, f32[9,16,128]{2,1,0:T(8,128)S(1)}, f32...) custom-call(f32[128,512]{1,0:T(8,128)S(1)} %collective-permute-done.1.g_even, ...), custom_call_target="tpu_custom_call" | custom-call | flops 150994944 | bytes 1048576 | tf_op jit(solution)/shard_map/pallas_call | solution.py:337
  27.1 1.8 %collective-permute-start.13 = (f32[2,9,16,128]{3,2,1,0:T(8,128)S(1)}, f32[2,9,16,128]{3,2,1,0:T(8,128)S(1)}, u32[]{:S(2)}, u32[]{:S(2)}) collective-permute-start(f32[2,9,16,128]{3,2,1,0:T(8,128)S(1)} %get-tuple-element.58), channel_id=1, source_target_pairs={{0,8},{2,10},{4,12},{6,14},{8,0},{10,2},{12,4},{14,6},{16,24},{18,... | collective-permute-start | bytes 442376 | tf_op jit(solution)/shard_map/ppermute | solution.py:251
  29.2 3.0 %collective-permute-start.11 = (f32[9,16,128]{2,1,0:T(8,128)S(1)}, f32[9,16,128]{2,1,0:T(8,128)S(1)}, u32[]{:S(2)}, u32[]{:S(2)}) collective-permute-start(f32[9,16,128]{2,1,0:T(8,128)S(1)} %get-tuple-element.55), channel_id=1, source_target_pairs={{0,16},{2,18},{4,20},{6,22},{8,24},{10,26},{12,28},{14,30},{16,0},... | collective-permute-start | bytes 221192 | tf_op jit(solution)/shard_map/ppermute | solution.py:251
  32.3 1.1 %collective-permute-start.12 = (f32[9,16,128]{2,1,0:T(8,128)S(1)}, f32[9,16,128]{2,1,0:T(8,128)S(1)}, u32[]{:S(2)}, u32[]{:S(2)}) collective-permute-start(f32[9,16,128]{2,1,0:T(8,128)S(1)} %get-tuple-element.56), channel_id=1, source_target_pairs={{0,24},{2,26},{4,28},{6,30},{8,16},{10,18},{12,20},{14,22},{16,8},... | collective-permute-start | bytes 221192 | tf_op jit(solution)/shard_map/ppermute | solution.py:251
  33.4 1.6 %collective-permute-start.14 = (f32[9,16,128]{2,1,0:T(8,128)S(1)}, f32[9,16,128]{2,1,0:T(8,128)S(1)}, u32[]{:S(2)}, u32[]{:S(2)}) collective-permute-start(f32[9,16,128]{2,1,0:T(8,128)S(1)} %get-tuple-element.59), channel_id=1, source_target_pairs={{0,4},{2,6},{4,0},{6,2},{8,12},{10,14},{12,8},{14,10},{16,20},{18,... | collective-permute-start | bytes 221192 | tf_op jit(solution)/shard_map/ppermute | solution.py:251
  34.9 3.4 %collective-permute-start.15 = (f32[9,16,128]{2,1,0:T(8,128)S(1)}, f32[9,16,128]{2,1,0:T(8,128)S(1)}, u32[]{:S(2)}, u32[]{:S(2)}) collective-permute-start(f32[9,16,128]{2,1,0:T(8,128)S(1)} %get-tuple-element.60), channel_id=1, source_target_pairs={{0,20},{2,22},{4,16},{6,18},{8,28},{10,30},{12,24},{14,26},{16,4},... | collective-permute-start | bytes 221192 | tf_op jit(solution)/shard_map/ppermute | solution.py:251
  38.3 0.7 %collective-permute-done.12.refs_3_ = f32[9,16,128]{2,1,0:T(8,128)S(1)} collective-permute-done((f32[9,16,128]{2,1,0:T(8,128)S(1)}, f32[9,16,128]{2,1,0:T(8,128)S(1)}, u32[]{:S(2)}, u32[]{:S(2)}) %collective-permute-start.12) | collective-permute-done | bytes 73760 | tf_op jit(solution)/shard_map/ppermute | solution.py:251
  39.0 2.1 %collective-permute-done.15.refs_5_ = f32[9,16,128]{2,1,0:T(8,128)S(1)} collective-permute-done((f32[9,16,128]{2,1,0:T(8,128)S(1)}, f32[9,16,128]{2,1,0:T(8,128)S(1)}, u32[]{:S(2)}, u32[]{:S(2)}) %collective-permute-start.15) | collective-permute-done | bytes 73760 | tf_op jit(solution)/shard_map/ppermute | solution.py:251
  41.1 2.0 %all_gather.7.sums_ref = f32[2,18,16,128]{3,2,1,0:T(8,128)S(1)} all-gather(f32[1,18,16,128]{3,2,1,0:T(8,128)S(1)} %shard_map.64), channel_id=1, replica_groups=mesh['wide'=16,'narrow'=2] {'narrow'}, dimensions={0}, use_global_device_ids=true | all-gather | bytes 442368 | tf_op jit(solution)/shard_map/all_gather | solution.py:359
  43.1 1.1 %shard_map.65 = f32[4,16,2304]{2,1,0:T(8,128)} custom-call(f32[2,18,16,128]{3,2,1,0:T(8,128)S(1)} %all_gather.7.sums_ref, f32[2,16,128]{2,1,0:T(8,128)S(1)} %bitcast.3, f32[2,16,2304]{2,1,0:T(8,128)S(1)} %get-tuple-element.61.mixed_ref, f32[2,16,128]{2,1,0:T(8,128)S(1)} %get-tuple-element.62.scale_ref), custom_call_target="tpu_custom_call" | custom-call | bytes 1048576 | tf_op jit(solution)/shard_map/pallas_call | solution.py:360
  (31 shorter events, 2.9 us)
Async XLA Ops:
  0.0 4.2 %copy-start.1 = (f32[1,1,512,256]{3,2,1,0:T(8,128)S(1)}, f32[1,1,512,256]{3,2,1,0:T(8,128)}, u32[]{:S(2)}) copy-start(f32[1,1,512,256]{3,2,1,0:T(8,128)} %g_ref.1) | copy-start | bytes 1572868
  0.0 1.1 %copy-start.3 = (f32[1,1,512,256]{3,2,1,0:T(8,128)S(1)}, f32[1,1,512,256]{3,2,1,0:T(8,128)}, u32[]{:S(2)}) copy-start(f32[1,1,512,256]{3,2,1,0:T(8,128)} %f_ref.1) | copy-start | bytes 1572868
  1.1 5.5 %copy-start.2 = (s32[16,4]{0,1:T(4,128)S(1)}, s32[16,4]{0,1:T(4,128)}, u32[]{:S(2)}) copy-start(s32[16,4]{0,1:T(4,128)} %param.8) | copy-start | bytes 772
  1.1 7.9 %copy-start = (f32[4,16,2304]{2,1,0:T(8,128)S(1)}, f32[4,16,2304]{2,1,0:T(8,128)}, u32[]{:S(2)}) copy-start(f32[4,16,2304]{2,1,0:T(8,128)} %bank_ref.1) | copy-start | bytes 1769476
  1.2 9.4 %collective-permute-start.3 = (f32[512,128]{1,0:T(8,128)S(1)}, f32[512,128]{1,0:T(8,128)S(1)}, u32[]{:S(2)}, u32[]{:S(2)}) collective-permute-start(f32[512,128]{1,0:T(8,128)S(1)} %get-tuple-element.38), channel_id=1, source_target_pairs={{0,4},{2,6},{4,0},{6,2},{8,12},{10,14},{12,8},{14,10},{16,20},{18,... | collective-permute-start | bytes 786440 | tf_op jit(solution)/shard_map/ppermute | solution.py:251
  4.4 8.0 %collective-permute-start.5 = (f32[128,512]{1,0:T(8,128)S(1)}, f32[128,512]{1,0:T(8,128)S(1)}, u32[]{:S(2)}, u32[]{:S(2)}) collective-permute-start(f32[128,512]{1,0:T(8,128)S(1)} %get-tuple-element.34.after_ref), channel_id=1, source_target_pairs={{0,2},{2,0},{4,6},{6,4},{8,10},{10,8},{12,14},{14,12},{16,18},{18,... | collective-permute-start | bytes 786440 | tf_op jit(solution)/shard_map/ppermute | solution.py:251
  9.3 8.4 %collective-permute-start = (f32[128,512]{1,0:T(8,128)S(1)}, f32[128,512]{1,0:T(8,128)S(1)}, u32[]{:S(2)}, u32[]{:S(2)}) collective-permute-start(f32[128,512]{1,0:T(8,128)S(1)} %get-tuple-element.37.g_own), channel_id=1, source_target_pairs={{0,4},{2,6},{4,0},{6,2},{8,12},{10,14},{12,8},{14,10},{16,20},{18,... | collective-permute-start | bytes 786440 | tf_op jit(solution)/shard_map/ppermute | solution.py:251
  9.8 9.2 %collective-permute-start.7 = (f32[512,128]{1,0:T(8,128)S(1)}, f32[512,128]{1,0:T(8,128)S(1)}, u32[]{:S(2)}, u32[]{:S(2)}) collective-permute-start(f32[512,128]{1,0:T(8,128)S(1)} %get-tuple-element.39.f_own), channel_id=1, source_target_pairs={{0,2},{2,0},{4,6},{6,4},{8,10},{10,8},{12,14},{14,12},{16,18},{18,... | collective-permute-start | bytes 786440 | tf_op jit(solution)/shard_map/ppermute | solution.py:251
  10.6 10.0 %collective-permute-start.8 = (f32[512,128]{1,0:T(8,128)S(1)}, f32[512,128]{1,0:T(8,128)S(1)}, u32[]{:S(2)}, u32[]{:S(2)}) collective-permute-start(f32[512,128]{1,0:T(8,128)S(1)} %broadcast_select_fusion), channel_id=1, source_target_pairs={{0,8},{2,10},{4,12},{6,14},{8,0},{10,2},{12,4},{14,6},{16,24},{18,... | collective-permute-start | bytes 786440 | tf_op jit(solution)/shard_map/ppermute | solution.py:251
  12.4 9.3 %collective-permute-start.9 = (f32[512,128]{1,0:T(8,128)S(1)}, f32[512,128]{1,0:T(8,128)S(1)}, u32[]{:S(2)}, u32[]{:S(2)}) collective-permute-start(f32[512,128]{1,0:T(8,128)S(1)} %broadcast_select_fusion), channel_id=1, source_target_pairs={{0,1},{1,0},{2,3},{3,2},{4,5},{5,4},{6,7},{7,6},{8,16},{9,17},{10,... | collective-permute-start | bytes 786440 | tf_op jit(solution)/shard_map/ppermute | solution.py:251
  12.4 11.1 %collective-permute-start.4 = (f32[512,128]{1,0:T(8,128)S(1)}, f32[512,128]{1,0:T(8,128)S(1)}, u32[]{:S(2)}, u32[]{:S(2)}) collective-permute-start(f32[512,128]{1,0:T(8,128)S(1)} %collective-permute-done.3.f_yn), channel_id=1, source_target_pairs={{0,2},{2,0},{4,6},{6,4},{8,10},{10,8},{12,14},{14,12},{16,18},{18,... | collective-permute-start | bytes 786440 | tf_op jit(solution)/shard_map/ppermute | solution.py:251
  17.7 7.5 %collective-permute-start.6 = (f32[128,512]{1,0:T(8,128)S(1)}, f32[128,512]{1,0:T(8,128)S(1)}, u32[]{:S(2)}, u32[]{:S(2)}) collective-permute-start(f32[128,512]{1,0:T(8,128)S(1)} %collective-permute-done.5.g_xn), channel_id=1, source_target_pairs={{0,4},{2,6},{4,0},{6,2},{8,12},{10,14},{12,8},{14,10},{16,20},{18,... | collective-permute-start | bytes 786440 | tf_op jit(solution)/shard_map/ppermute | solution.py:251
  19.0 7.5 %collective-permute-start.1 = (f32[128,512]{1,0:T(8,128)S(1)}, f32[128,512]{1,0:T(8,128)S(1)}, u32[]{:S(2)}, u32[]{:S(2)}) collective-permute-start(f32[128,512]{1,0:T(8,128)S(1)} %broadcast_select_fusion.1), channel_id=1, source_target_pairs={{0,8},{2,10},{4,12},{6,14},{8,0},{10,2},{12,4},{14,6},{16,24},{18,... | collective-permute-start | bytes 786440 | tf_op jit(solution)/shard_map/ppermute | solution.py:251
  20.6 5.9 %collective-permute-start.2 = (f32[128,512]{1,0:T(8,128)S(1)}, f32[128,512]{1,0:T(8,128)S(1)}, u32[]{:S(2)}, u32[]{:S(2)}) collective-permute-start(f32[128,512]{1,0:T(8,128)S(1)} %broadcast_select_fusion.1), channel_id=1, source_target_pairs={{0,1},{1,0},{2,3},{3,2},{4,5},{5,4},{6,7},{7,6},{8,16},{9,17},{10,... | collective-permute-start | bytes 786440 | tf_op jit(solution)/shard_map/ppermute | solution.py:251
  27.1 6.2 %collective-permute-start.13 = (f32[2,9,16,128]{3,2,1,0:T(8,128)S(1)}, f32[2,9,16,128]{3,2,1,0:T(8,128)S(1)}, u32[]{:S(2)}, u32[]{:S(2)}) collective-permute-start(f32[2,9,16,128]{3,2,1,0:T(8,128)S(1)} %get-tuple-element.58), channel_id=1, source_target_pairs={{0,8},{2,10},{4,12},{6,14},{8,0},{10,2},{12,4},{14,6},{16,24},{18,... | collective-permute-start | bytes 442376 | tf_op jit(solution)/shard_map/ppermute | solution.py:251
  28.9 9.4 %collective-permute-start.10 = (f32[9,16,128]{2,1,0:T(8,128)S(1)}, f32[9,16,128]{2,1,0:T(8,128)S(1)}, u32[]{:S(2)}, u32[]{:S(2)}) collective-permute-start(f32[9,16,128]{2,1,0:T(8,128)S(1)} %get-tuple-element.54), channel_id=1, source_target_pairs={{0,8},{2,10},{4,12},{6,14},{8,0},{10,2},{12,4},{14,6},{16,24},{18,... | collective-permute-start | bytes 221192 | tf_op jit(solution)/shard_map/ppermute | solution.py:251
  29.2 9.1 %collective-permute-start.11 = (f32[9,16,128]{2,1,0:T(8,128)S(1)}, f32[9,16,128]{2,1,0:T(8,128)S(1)}, u32[]{:S(2)}, u32[]{:S(2)}) collective-permute-start(f32[9,16,128]{2,1,0:T(8,128)S(1)} %get-tuple-element.55), channel_id=1, source_target_pairs={{0,16},{2,18},{4,20},{6,22},{8,24},{10,26},{12,28},{14,30},{16,0},... | collective-permute-start | bytes 221192 | tf_op jit(solution)/shard_map/ppermute | solution.py:251
  32.3 6.7 %collective-permute-start.12 = (f32[9,16,128]{2,1,0:T(8,128)S(1)}, f32[9,16,128]{2,1,0:T(8,128)S(1)}, u32[]{:S(2)}, u32[]{:S(2)}) collective-permute-start(f32[9,16,128]{2,1,0:T(8,128)S(1)} %get-tuple-element.56), channel_id=1, source_target_pairs={{0,24},{2,26},{4,28},{6,30},{8,16},{10,18},{12,20},{14,22},{16,8},... | collective-permute-start | bytes 221192 | tf_op jit(solution)/shard_map/ppermute | solution.py:251
  33.4 5.6 %collective-permute-start.14 = (f32[9,16,128]{2,1,0:T(8,128)S(1)}, f32[9,16,128]{2,1,0:T(8,128)S(1)}, u32[]{:S(2)}, u32[]{:S(2)}) collective-permute-start(f32[9,16,128]{2,1,0:T(8,128)S(1)} %get-tuple-element.59), channel_id=1, source_target_pairs={{0,4},{2,6},{4,0},{6,2},{8,12},{10,14},{12,8},{14,10},{16,20},{18,... | collective-permute-start | bytes 221192 | tf_op jit(solution)/shard_map/ppermute | solution.py:251
  34.9 6.2 %collective-permute-start.15 = (f32[9,16,128]{2,1,0:T(8,128)S(1)}, f32[9,16,128]{2,1,0:T(8,128)S(1)}, u32[]{:S(2)}, u32[]{:S(2)}) collective-permute-start(f32[9,16,128]{2,1,0:T(8,128)S(1)} %get-tuple-element.60), channel_id=1, source_target_pairs={{0,20},{2,22},{4,16},{6,18},{8,28},{10,30},{12,24},{14,26},{16,4},... | collective-permute-start | bytes 221192 | tf_op jit(solution)/shard_map/ppermute | solution.py:251

commit v3 on v2

--- a/solution.py
+++ b/solution.py
@@ -59,7 +59,7 @@
         g_send[rows] = jnp.where(x == 0, high, low)
 
 
-def mix_body(every_ref, bank_ref, f_in, g_in, mixed_ref, scale_ref, f_out, g_out):
+def mix_body(every_ref, bank_ref, mixed_ref, scale_ref):
     samples, kinds = every_ref.shape[0], bank_ref.shape[0]
     for s in range(samples):
         mixed = every_ref[s, 0:1, 0:1] * bank_ref[0]
@@ -195,13 +195,13 @@
     rows = 2 * owned
     for m in range(groups):
         start = pl.multiple_of((group ^ m) * rows, rows)
-        across = (odds if m % 2 else evens).at[m // 2]
+        along = (odds if m % 2 else evens).at[m // 2]
         for a, sums in enumerate((side.at[0], mid, side.at[1])):
             for b in range(3):
                 both = sums[pl.ds(b * n_out + start, rows), :]
                 low, high = both[:owned], both[owned:]
-                outs[m][3 * a + b] = jnp.where(y == 0, low, high)
-                across[3 * a + b] = jnp.where(y == 0, high, low)
+                outs[m][3 * a + b] = jnp.where(y == 0, high, low)
+                along[3 * a + b] = jnp.where(y == 0, low, high)
 
 
 def pair_body(*refs):
@@ -210,36 +210,36 @@
         out[...] = mine[k] + theirs[k]
 
 
-def sum_body(groups, *refs):
-    parts, out = refs[:-1], refs[-1]
-    taps = parts[0].shape[0]
-    for d, terms in enumerate((parts[:groups], parts[groups:])):
-        for t in range(taps):
-            total = terms[0][t]
-            for term in terms[1:]:
-                total = total + term[t]
-            out[0, d * taps + t] = total
-
-
-def final_body(sums_ref, every_ref, mixed_ref, scale_ref, out_ref, held, sem):
+def sum_body(*refs):
+    terms, out = refs[:-1], refs[-1]
+    for t in range(out.shape[0]):
+        total = terms[0][t]
+        for term in terms[1:]:
+            total = total + term[t]
+        out[t] = total
+
+
+def final_body(kept_own, kept_more, got_own, got_more, every_ref, mixed_ref, scale_ref, out_ref, held, sem):
     _, _, _, y = place()
-    samples, taps = sums_ref.shape[0], sums_ref.shape[1] // 2
+    samples, taps = every_ref.shape[0], kept_own.shape[0]
     kinds = held.shape[0]
-    grads = []
+    grads, weights = [], []
     for s in range(samples):
+        kept = kept_own if s == 0 else kept_more.at[s - 1]
+        got = got_own if s == 0 else got_more.at[s - 1]
         pieces = []
         for t in range(taps):
-            kept, got = sums_ref[s, t], sums_ref[s, taps + t]
-            pieces += [jnp.where(y == 0, kept, got), jnp.where(y == 0, got, kept)]
+            pieces += [jnp.where(y == 0, kept[t], got[t]), jnp.where(y == 0, got[t], kept[t])]
         grad = jnp.concatenate(pieces, axis=1)
         mixed, scale = mixed_ref[s], scale_ref[s, :, 0:1]
         inner = jnp.sum(mixed * grad, axis=1, keepdims=True)
         grads.append(scale * grad - (scale * scale * scale * inner) * mixed)
+        weights.append(every_ref[s])
     copies = []
     for k in range(kinds):
-        total = every_ref[0, k : k + 1, 0:1] * grads[0]
+        total = weights[0][k : k + 1, 0:1] * grads[0]
         for s in range(1, samples):
-            total = total + every_ref[s, k : k + 1, 0:1] * grads[s]
+            total = total + weights[s][k : k + 1, 0:1] * grads[s]
         held[k] = total
         copies.append(pltpu.make_async_copy(held.at[k], out_ref.at[k], sem.at[k]))
         copies[-1].start()
@@ -283,15 +283,13 @@
 
     f_yn = send(f_send, over_y)
     g_xn = send(g_send, over_x)
-    every_mix = lax.all_gather(mix[None], "narrow", axis=0, tiled=True)
+
+    def others(value):
+        return [send(value, [((c + s) % cores, c) for c in range(cores)], "narrow") for s in range(1, cores)]
+
+    every_mix = jnp.stack([mix] + others(mix))
     samples = every_mix.shape[0]
-    mixed, scale, f_keep, g_keep = call(
-        mix_body,
-        (shape(samples, *bank.shape[1:]), shape(samples, owned, 128), f_shape, g_shape),
-        "vvaa",
-        (VMEM_SPEC, VMEM_SPEC, ANY_SPEC, ANY_SPEC),
-        alias={2: 2, 3: 3},
-    )(every_mix, bank, f_keep, g_keep)
+    mixed, scale = call(mix_body, (shape(samples, *bank.shape[1:]), shape(samples, owned, 128)), "vv")(every_mix, bank)
     f_xn = send(f_keep, over_x)
     g_yn = send(g_keep, over_y)
     f_dg = send(f_yn, over_x)
@@ -320,17 +318,10 @@
         first_body, (mids, sides, lefts(2), lefts(2), rights(2)), "vvvv", flops=3 * pair
     )(f_keep, f_yn, g_keep, g_xn)
     mid, side, *more = call(
-        functools.partial(near_body, groups),
-        (mids, sides, lefts(1), lefts(1), rights(2)),
-        "v" * 9,
-        flops=4 * pair,
+        functools.partial(near_body, groups), (mids, sides, lefts(1), lefts(1), rights(2)), "v" * 9, flops=4 * pair
     )(f_xn, g_yn, f_even, f_odd, mid, side, lh, ll, rt)
     mid, side, rt_far = call(
-        far_body,
-        (mids, sides, rights(1)),
-        "v" * 10,
-        flops=5 * pair,
-        scratch=[pltpu.VMEM(lefts(1).shape, BF16)] * 2,
+        far_body, (mids, sides, rights(1)), "v" * 10, flops=5 * pair, scratch=[pltpu.VMEM(lefts(1).shape, BF16)] * 2
     )(f_dg, g_dg, mid, side, lh, ll, rt, *more)
     piece = shape(9, owned, half_in)
     stack = shape(groups // 2, *piece.shape)
@@ -350,20 +341,20 @@
         return [(i, i ^ (4 * m + 2 * d)) for i in everyone]
 
     theirs = send(odds, hop(1, 0))
-    parts = [blocks[0]] + [send(blocks[m], hop(m, 0)) for m in range(1, groups)]
+    parts = [send(blocks[m], hop(m, 1)) for m in range(groups)]
     pairs = call(pair_body, [piece] * (groups // 2), "vv")(evens, theirs)
-    parts += [send(pairs[k], hop(2 * k, 1)) for k in range(groups // 2)]
-    own_sums = call(
-        functools.partial(sum_body, groups), shape(1, 18, owned, half_in), "v" * len(parts)
-    )(*parts)
-    every_sum = lax.all_gather(own_sums, "narrow", axis=0, tiled=True)
+    parts += [pairs[0]]
+    parts += [send(pairs[k], hop(2 * k, 0)) for k in range(1, groups // 2)]
+    got = call(sum_body, piece, "v" * groups)(*parts[:groups])
+    kept = call(sum_body, piece, "v" * (groups // 2))(*parts[groups:])
+
     return call(
         final_body,
         shape(*bank.shape),
-        "vvvv",
+        "v" * 7,
         ANY_SPEC,
         scratch=(pltpu.VMEM(bank.shape, F32), pltpu.SemaphoreType.DMA((bank.shape[0],))),
-    )(every_sum, every_mix, mixed, scale)
+    )(kept, jnp.stack(others(kept)), got, jnp.stack(others(got)), every_mix, mixed, scale)
 
 
 def solution(mesh):

time: 44.6 us -> 45.2 us (1.013)
  waiting for transfers between devices: 9.03 us -> 13.5 us
  blocking collectives: 3.84 us -> 0 us
    ppermute x16 -> x19, waiting for transfers between devices: 9.03 us -> 13.5 us  [send(): return lax.ppermute(value, axes, pairs)]
    all_gather x2 -> x0, blocking collectives: 3.84 us -> none  [the longest x1 2.02 us: local(): every_sum = lax.all_gather(own_sums, 'narrow', axis=0, tiled=True)]
    ppermute x16 -> x19, starting transfers between devices: 22.7 us -> 23 us  [send(): return lax.ppermute(value, axes, pairs)]
    pallas_call x2 -> x3, Pallas kernels: 1.13 us -> 1.14 us  [the longest x1 1.11 us: local(): call(final_body, shape(*bank.shape), 'v' * 7, ANY_SPEC, scratch=(pltpu.VM...]
  transfers between devices with their start and end apart: 16 -> 19, of which waited for: 7 -> 10; matrix products, arithmetic and copies ran while one was open for 0% -> 0% of each run, Pallas kernels for 11% -> 11%
where the time goes in v3:
time: 45.2 us; the launch traced here: 45.1 us
  starting transfers between devices  23 us (51%)
  waiting for transfers between devices  13.5 us (30%)
  Pallas kernels  6.66 us (15%)
  local copies, waits for them, and re-layouts  1.11 us (2%)
  between operations  0.82 us (2%)
    ppermute x19, starting transfers between devices, send(): return lax.ppermute(value, axes, pairs)  23 us
    ppermute x19, waiting for transfers between devices, send(): return lax.ppermute(value, axes, pairs)  13.5 us
    pallas_call x1, Pallas kernels, local(): call(functools.partial(near_body, groups), (mids, sides, lefts(1), lefts(...  1.47 us
    pallas_call x1, Pallas kernels, local(): call(far_body, (mids, sides, rights(1)), 'v' * 10, flops=5 * pair, scratc...  1.26 us
    pallas_call x1, Pallas kernels, local(): call(first_body, (mids, sides, lefts(2), lefts(2), rights(2)), 'vvvv', fl...  1.11 us
    unnamed x8, local copies, waits for them, and re-layouts  1.11 us
    pallas_call x1, Pallas kernels, local(): call(final_body, shape(*bank.shape), 'v' * 7, ANY_SPEC, scratch=(pltpu.VM...  1.11 us
  transfers between devices with their start and end apart: 19, of which 10 were waited for; matrix products, arithmetic and copies ran while one was open for 0% of the time, Pallas kernels for 11%

profile of v3, /device:TPU:0, one launch (start us, length us, event | category | flops | bytes accessed | tf_op | source)
XLA Modules:
  0.0 45.1 jit_solution(12585336430168716420)
XLA Ops:
  0.0 1.1 %copy-done.3 = f32[1,1,512,256]{3,2,1,0:T(8,128)S(1)} copy-done((f32[1,1,512,256]{3,2,1,0:T(8,128)S(1)}, f32[1,1,512,256]{3,2,1,0:T(8,128)}, u32[]{:S(2)}) %copy-start.3) | copy-done | bytes 524312
  1.1 3.1 %collective-permute-start.3 = (f32[512,128]{1,0:T(8,128)S(1)}, f32[512,128]{1,0:T(8,128)S(1)}, u32[]{:S(2)}, u32[]{:S(2)}) collective-permute-start(f32[512,128]{1,0:T(8,128)S(1)} %get-tuple-element.33), channel_id=1, source_target_pairs={{0,4},{2,6},{4,0},{6,2},{8,12},{10,14},{12,8},{14,10},{16,20},{18,... | collective-permute-start | bytes 786440 | tf_op jit(solution)/shard_map/ppermute | solution.py:251
  4.4 1.6 %collective-permute-start.5 = (f32[128,512]{1,0:T(8,128)S(1)}, f32[128,512]{1,0:T(8,128)S(1)}, u32[]{:S(2)}, u32[]{:S(2)}) collective-permute-start(f32[128,512]{1,0:T(8,128)S(1)} %get-tuple-element.34.after_ref), channel_id=1, source_target_pairs={{0,2},{2,0},{4,6},{6,4},{8,10},{10,8},{12,14},{14,12},{16,18},{18,... | collective-permute-start | bytes 786440 | tf_op jit(solution)/shard_map/ppermute | solution.py:251
  6.5 4.8 %collective-permute-done.3.f_yn = f32[512,128]{1,0:T(8,128)S(1)} collective-permute-done((f32[512,128]{1,0:T(8,128)S(1)}, f32[512,128]{1,0:T(8,128)S(1)}, u32[]{:S(2)}, u32[]{:S(2)}) %collective-permute-start.3) | collective-permute-done | bytes 262176 | tf_op jit(solution)/shard_map/ppermute | solution.py:251
  11.4 2.1 %collective-permute-start.8 = (f32[512,128]{1,0:T(8,128)S(1)}, f32[512,128]{1,0:T(8,128)S(1)}, u32[]{:S(2)}, u32[]{:S(2)}) collective-permute-start(f32[512,128]{1,0:T(8,128)S(1)} %broadcast_select_fusion), channel_id=1, source_target_pairs={{0,8},{2,10},{4,12},{6,14},{8,0},{10,2},{12,4},{14,6},{16,24},{18,... | collective-permute-start | bytes 786440 | tf_op jit(solution)/shard_map/ppermute | solution.py:251
  13.6 1.5 %collective-permute-start.4 = (f32[512,128]{1,0:T(8,128)S(1)}, f32[512,128]{1,0:T(8,128)S(1)}, u32[]{:S(2)}, u32[]{:S(2)}) collective-permute-start(f32[512,128]{1,0:T(8,128)S(1)} %collective-permute-done.3.f_yn), channel_id=1, source_target_pairs={{0,2},{2,0},{4,6},{6,4},{8,10},{10,8},{12,14},{14,12},{16,18},{18,... | collective-permute-start | bytes 786440 | tf_op jit(solution)/shard_map/ppermute | solution.py:251
  15.1 1.0 %collective-permute-done.g_yn = f32[128,512]{1,0:T(8,128)S(1)} collective-permute-done((f32[128,512]{1,0:T(8,128)S(1)}, f32[128,512]{1,0:T(8,128)S(1)}, u32[]{:S(2)}, u32[]{:S(2)}) %collective-permute-start) | collective-permute-done | bytes 262176 | tf_op jit(solution)/shard_map/ppermute | solution.py:251
  16.1 1.7 %collective-permute-start.6 = (f32[128,512]{1,0:T(8,128)S(1)}, f32[128,512]{1,0:T(8,128)S(1)}, u32[]{:S(2)}, u32[]{:S(2)}) collective-permute-start(f32[128,512]{1,0:T(8,128)S(1)} %collective-permute-done.5.g_xn), channel_id=1, source_target_pairs={{0,4},{2,6},{4,0},{6,2},{8,12},{10,14},{12,8},{14,10},{16,20},{18,... | collective-permute-start | bytes 786440 | tf_op jit(solution)/shard_map/ppermute | solution.py:251
  17.9 1.2 %collective-permute-done.7.f_xn = f32[512,128]{1,0:T(8,128)S(1)} collective-permute-done((f32[512,128]{1,0:T(8,128)S(1)}, f32[512,128]{1,0:T(8,128)S(1)}, u32[]{:S(2)}, u32[]{:S(2)}) %collective-permute-start.7) | collective-permute-done | bytes 262176 | tf_op jit(solution)/shard_map/ppermute | solution.py:251
  19.1 1.8 %collective-permute-start.1 = (f32[128,512]{1,0:T(8,128)S(1)}, f32[128,512]{1,0:T(8,128)S(1)}, u32[]{:S(2)}, u32[]{:S(2)}) collective-permute-start(f32[128,512]{1,0:T(8,128)S(1)} %broadcast_select_fusion.1), channel_id=1, source_target_pairs={{0,8},{2,10},{4,12},{6,14},{8,0},{10,2},{12,4},{14,6},{16,24},{18,... | collective-permute-start | bytes 786440 | tf_op jit(solution)/shard_map/ppermute | solution.py:251
  20.8 1.1 %shard_map.57 = (f32[384,128]{1,0:T(8,128)S(1)}, f32[2,384,128]{2,1,0:T(8,128)S(1)}, bf16[2,384,512]{2,1,0:T(8,128)(2,1)S(1)}, bf16[2,384,512]{2,1,0:T(8,128)(2,1)S(1)}, bf16[2,512,256]{2,1,0:T(8,128)(2,1)S(1)}) custom-call(f32[512,128]{1,0:T(8,128)S(1)} %get-tuple-element.35.f_own, f32[512,128]{1,0:T(8,128)S(1)} %collective-permute-done.3.f_yn, ...), custom_call_target="tpu_custom_call" | custom-call | flops 452984832 | bytes 1048576 | tf_op jit(solution)/shard_map/pallas_call | solution.py:317
  22.0 1.5 %shard_map.58 = (f32[384,128]{1,0:T(8,128)S(1)}, f32[2,384,128]{2,1,0:T(8,128)S(1)}, bf16[1,384,512]{2,1,0:T(8,128)(2,1)S(1)}, bf16[1,384,512]{2,1,0:T(8,128)(2,1)S(1)}, bf16[2,512,256]{2,1,0:T(8,128)(2,1)S(1)}) custom-call(f32[512,128]{1,0:T(8,128)S(1)} %collective-permute-done.7.f_xn, f32[128,512]{1,0:T(8,128)S(1)} %collective-permute-done.g_yn, ...), custom_call_target="tpu_custom_call" | custom-call | flops 603979776 | bytes 1048576 | tf_op jit(solution)/shard_map/pallas_call | solution.py:320
  23.6 1.3 %shard_map.59 = (f32[384,128]{1,0:T(8,128)S(1)}, f32[2,384,128]{2,1,0:T(8,128)S(1)}, bf16[1,512,256]{2,1,0:T(8,128)(2,1)S(1)}) custom-call(f32[512,128]{1,0:T(8,128)S(1)} %collective-permute-done.4.f_dg, f32[128,512]{1,0:T(8,128)S(1)} %collective-permute-done.6.g_dg, f32[384,128]{1,0:T(8,128)S(1)} %get-tuple-element.41.mid_in, ...), custom_call_target="tpu_custom_call" | custom-call | flops 754974720 | bytes 1048576 | tf_op jit(solution)/shard_map/pallas_call | solution.py:323
  25.4 0.6 %shard_map.60 = (f32[9,16,128]{2,1,0:T(8,128)S(1)}, f32[9,16,128]{2,1,0:T(8,128)S(1)}, f32[9,16,128]{2,1,0:T(8,128)S(1)}, f32[9,16,128]{2,1,0:T(8,128)S(1)}, f32...) custom-call(f32[128,512]{1,0:T(8,128)S(1)} %collective-permute-done.1.g_even, ...), custom_call_target="tpu_custom_call" | custom-call | flops 150994944 | bytes 1048576 | tf_op jit(solution)/shard_map/pallas_call | solution.py:328
  26.1 3.0 %collective-permute-start.10 = (f32[2,9,16,128]{3,2,1,0:T(8,128)S(1)}, f32[2,9,16,128]{3,2,1,0:T(8,128)S(1)}, u32[]{:S(2)}, u32[]{:S(2)}) collective-permute-start(f32[2,9,16,128]{3,2,1,0:T(8,128)S(1)} %get-tuple-element.50), channel_id=1, source_target_pairs={{0,8},{2,10},{4,12},{6,14},{8,0},{10,2},{12,4},{14,6},{16,24},{18,... | collective-permute-start | bytes 442376 | tf_op jit(solution)/shard_map/ppermute | solution.py:251
  29.5 1.1 %collective-permute-start.14 = (f32[9,16,128]{2,1,0:T(8,128)S(1)}, f32[9,16,128]{2,1,0:T(8,128)S(1)}, u32[]{:S(2)}, u32[]{:S(2)}) collective-permute-start(f32[9,16,128]{2,1,0:T(8,128)S(1)} %get-tuple-element.54), channel_id=1, source_target_pairs={{0,12},{2,14},{4,8},{6,10},{8,4},{10,6},{12,0},{14,2},{16,28},{18,... | collective-permute-start | bytes 221192 | tf_op jit(solution)/shard_map/ppermute | solution.py:251
  30.6 3.3 %collective-permute-start.15 = (f32[9,16,128]{2,1,0:T(8,128)S(1)}, f32[9,16,128]{2,1,0:T(8,128)S(1)}, u32[]{:S(2)}, u32[]{:S(2)}) collective-permute-start(f32[9,16,128]{2,1,0:T(8,128)S(1)} %get-tuple-element.55), channel_id=1, source_target_pairs={{0,20},{2,22},{4,16},{6,18},{8,28},{10,30},{12,24},{14,26},{16,4},... | collective-permute-start | bytes 221192 | tf_op jit(solution)/shard_map/ppermute | solution.py:251
  33.9 1.9 %collective-permute-start.16 = (f32[9,16,128]{2,1,0:T(8,128)S(1)}, f32[9,16,128]{2,1,0:T(8,128)S(1)}, u32[]{:S(2)}, u32[]{:S(2)}) collective-permute-start(f32[9,16,128]{2,1,0:T(8,128)S(1)} %get-tuple-element.56), channel_id=1, source_target_pairs={{0,28},{2,30},{4,24},{6,26},{8,20},{10,22},{12,16},{14,18},{16,12}... | collective-permute-start | bytes 221192 | tf_op jit(solution)/shard_map/ppermute | solution.py:251
  35.8 0.7 %collective-permute-start.11 = (f32[9,16,128]{2,1,0:T(8,128)S(1)}, f32[9,16,128]{2,1,0:T(8,128)S(1)}, u32[]{:S(2)}, u32[]{:S(2)}) collective-permute-start(f32[9,16,128]{2,1,0:T(8,128)S(1)} %get-tuple-element.52), channel_id=1, source_target_pairs={{0,16},{2,18},{4,20},{6,22},{8,24},{10,26},{12,28},{14,30},{16,0},... | collective-permute-start | bytes 221192 | tf_op jit(solution)/shard_map/ppermute | solution.py:251
  37.9 1.3 %collective-permute-done.15.refs_2_ = f32[9,16,128]{2,1,0:T(8,128)S(1)} collective-permute-done((f32[9,16,128]{2,1,0:T(8,128)S(1)}, f32[9,16,128]{2,1,0:T(8,128)S(1)}, u32[]{:S(2)}, u32[]{:S(2)}) %collective-permute-start.15) | collective-permute-done | bytes 73760 | tf_op jit(solution)/shard_map/ppermute | solution.py:251
  39.2 1.8 %collective-permute-done.16.refs_3_ = f32[9,16,128]{2,1,0:T(8,128)S(1)} collective-permute-done((f32[9,16,128]{2,1,0:T(8,128)S(1)}, f32[9,16,128]{2,1,0:T(8,128)S(1)}, u32[]{:S(2)}, u32[]{:S(2)}) %collective-permute-start.16) | collective-permute-done | bytes 73760 | tf_op jit(solution)/shard_map/ppermute | solution.py:251
  41.1 1.5 %collective-permute-done.11.refs_1_ = f32[9,16,128]{2,1,0:T(8,128)S(1)} collective-permute-done((f32[9,16,128]{2,1,0:T(8,128)S(1)}, f32[9,16,128]{2,1,0:T(8,128)S(1)}, u32[]{:S(2)}, u32[]{:S(2)}) %collective-permute-start.11) | collective-permute-done | bytes 73760 | tf_op jit(solution)/shard_map/ppermute | solution.py:251
  43.0 1.0 %collective-permute-done.12 = f32[9,16,128]{2,1,0:T(8,128)S(1)} collective-permute-done((f32[9,16,128]{2,1,0:T(8,128)S(1)}, f32[9,16,128]{2,1,0:T(8,128)S(1)}, u32[]{:S(2)}, u32[]{:S(2)}) %collective-permute-start.12) | collective-permute-done | bytes 73760 | tf_op jit(solution)/shard_map/ppermute | solution.py:251
  44.0 1.1 %shard_map.66 = f32[4,16,2304]{2,1,0:T(8,128)} custom-call(f32[9,16,128]{2,1,0:T(8,128)S(1)} %shard_map.62.kept_own, f32[1,9,16,128]{3,2,1,0:T(8,128)S(1)} %bitcast.6, f32[9,16,128]{2,1,0:T(8,128)S(1)} %shard_map.63.got_own, f32[1,9,16,128]{3,2,1,0:T(8,128)S(1)} %bitcast.5, f32[2,16,128]{2,1,0:T(8,128)S(1)} %pad_maximum_fusion.every_ref, ...), custom_call_target="tpu_custom_call" | custom-call | bytes 1048576 | tf_op jit(solution)/shard_map/pallas_call | solution.py:351
  (37 shorter events, 3.2 us)
Async XLA Ops:
  0.0 4.2 %copy-start.1 = (f32[1,1,512,256]{3,2,1,0:T(8,128)S(1)}, f32[1,1,512,256]{3,2,1,0:T(8,128)}, u32[]{:S(2)}) copy-start(f32[1,1,512,256]{3,2,1,0:T(8,128)} %g_ref.1) | copy-start | bytes 1572868
  0.0 1.1 %copy-start.3 = (f32[1,1,512,256]{3,2,1,0:T(8,128)S(1)}, f32[1,1,512,256]{3,2,1,0:T(8,128)}, u32[]{:S(2)}) copy-start(f32[1,1,512,256]{3,2,1,0:T(8,128)} %f_ref.1) | copy-start | bytes 1572868
  1.1 10.2 %collective-permute-start.3 = (f32[512,128]{1,0:T(8,128)S(1)}, f32[512,128]{1,0:T(8,128)S(1)}, u32[]{:S(2)}, u32[]{:S(2)}) collective-permute-start(f32[512,128]{1,0:T(8,128)S(1)} %get-tuple-element.33), channel_id=1, source_target_pairs={{0,4},{2,6},{4,0},{6,2},{8,12},{10,14},{12,8},{14,10},{16,20},{18,... | collective-permute-start | bytes 786440 | tf_op jit(solution)/shard_map/ppermute | solution.py:251
  4.4 9.2 %collective-permute-start.5 = (f32[128,512]{1,0:T(8,128)S(1)}, f32[128,512]{1,0:T(8,128)S(1)}, u32[]{:S(2)}, u32[]{:S(2)}) collective-permute-start(f32[128,512]{1,0:T(8,128)S(1)} %get-tuple-element.34.after_ref), channel_id=1, source_target_pairs={{0,2},{2,0},{4,6},{6,4},{8,10},{10,8},{12,14},{14,12},{16,18},{18,... | collective-permute-start | bytes 786440 | tf_op jit(solution)/shard_map/ppermute | solution.py:251
  6.0 10.2 %collective-permute-start = (f32[128,512]{1,0:T(8,128)S(1)}, f32[128,512]{1,0:T(8,128)S(1)}, u32[]{:S(2)}, u32[]{:S(2)}) collective-permute-start(f32[128,512]{1,0:T(8,128)S(1)} %get-tuple-element.32.g_own), channel_id=1, source_target_pairs={{0,4},{2,6},{4,0},{6,2},{8,12},{10,14},{12,8},{14,10},{16,20},{18,... | collective-permute-start | bytes 786440 | tf_op jit(solution)/shard_map/ppermute | solution.py:251
  6.5 12.6 %collective-permute-start.7 = (f32[512,128]{1,0:T(8,128)S(1)}, f32[512,128]{1,0:T(8,128)S(1)}, u32[]{:S(2)}, u32[]{:S(2)}) collective-permute-start(f32[512,128]{1,0:T(8,128)S(1)} %get-tuple-element.35.f_own), channel_id=1, source_target_pairs={{0,2},{2,0},{4,6},{6,4},{8,10},{10,8},{12,14},{14,12},{16,18},{18,... | collective-permute-start | bytes 786440 | tf_op jit(solution)/shard_map/ppermute | solution.py:251
  11.4 9.5 %collective-permute-start.8 = (f32[512,128]{1,0:T(8,128)S(1)}, f32[512,128]{1,0:T(8,128)S(1)}, u32[]{:S(2)}, u32[]{:S(2)}) collective-permute-start(f32[512,128]{1,0:T(8,128)S(1)} %broadcast_select_fusion), channel_id=1, source_target_pairs={{0,8},{2,10},{4,12},{6,14},{8,0},{10,2},{12,4},{14,6},{16,24},{18,... | collective-permute-start | bytes 786440 | tf_op jit(solution)/shard_map/ppermute | solution.py:251
  13.5 8.4 %collective-permute-start.9 = (f32[512,128]{1,0:T(8,128)S(1)}, f32[512,128]{1,0:T(8,128)S(1)}, u32[]{:S(2)}, u32[]{:S(2)}) collective-permute-start(f32[512,128]{1,0:T(8,128)S(1)} %broadcast_select_fusion), channel_id=1, source_target_pairs={{0,1},{1,0},{2,3},{3,2},{4,5},{5,4},{6,7},{7,6},{8,16},{9,17},{10,... | collective-permute-start | bytes 786440 | tf_op jit(solution)/shard_map/ppermute | solution.py:251
  13.6 9.8 %collective-permute-start.4 = (f32[512,128]{1,0:T(8,128)S(1)}, f32[512,128]{1,0:T(8,128)S(1)}, u32[]{:S(2)}, u32[]{:S(2)}) collective-permute-start(f32[512,128]{1,0:T(8,128)S(1)} %collective-permute-done.3.f_yn), channel_id=1, source_target_pairs={{0,2},{2,0},{4,6},{6,4},{8,10},{10,8},{12,14},{14,12},{16,18},{18,... | collective-permute-start | bytes 786440 | tf_op jit(solution)/shard_map/ppermute | solution.py:251
  16.1 7.5 %collective-permute-start.6 = (f32[128,512]{1,0:T(8,128)S(1)}, f32[128,512]{1,0:T(8,128)S(1)}, u32[]{:S(2)}, u32[]{:S(2)}) collective-permute-start(f32[128,512]{1,0:T(8,128)S(1)} %collective-permute-done.5.g_xn), channel_id=1, source_target_pairs={{0,4},{2,6},{4,0},{6,2},{8,12},{10,14},{12,8},{14,10},{16,20},{18,... | collective-permute-start | bytes 786440 | tf_op jit(solution)/shard_map/ppermute | solution.py:251
  19.1 6.4 %collective-permute-start.1 = (f32[128,512]{1,0:T(8,128)S(1)}, f32[128,512]{1,0:T(8,128)S(1)}, u32[]{:S(2)}, u32[]{:S(2)}) collective-permute-start(f32[128,512]{1,0:T(8,128)S(1)} %broadcast_select_fusion.1), channel_id=1, source_target_pairs={{0,8},{2,10},{4,12},{6,14},{8,0},{10,2},{12,4},{14,6},{16,24},{18,... | collective-permute-start | bytes 786440 | tf_op jit(solution)/shard_map/ppermute | solution.py:251
  20.8 4.6 %collective-permute-start.2 = (f32[128,512]{1,0:T(8,128)S(1)}, f32[128,512]{1,0:T(8,128)S(1)}, u32[]{:S(2)}, u32[]{:S(2)}) collective-permute-start(f32[128,512]{1,0:T(8,128)S(1)} %broadcast_select_fusion.1), channel_id=1, source_target_pairs={{0,1},{1,0},{2,3},{3,2},{4,5},{5,4},{6,7},{7,6},{8,16},{9,17},{10,... | collective-permute-start | bytes 786440 | tf_op jit(solution)/shard_map/ppermute | solution.py:251
  25.4 11.8 %copy-start.2 = (s32[16,4]{0,1:T(4,128)S(1)}, s32[16,4]{0,1:T(4,128)}, u32[]{:S(2)}) copy-start(s32[16,4]{0,1:T(4,128)} %param.8) | copy-start | bytes 772
  26.1 9.7 %collective-permute-start.10 = (f32[2,9,16,128]{3,2,1,0:T(8,128)S(1)}, f32[2,9,16,128]{3,2,1,0:T(8,128)S(1)}, u32[]{:S(2)}, u32[]{:S(2)}) collective-permute-start(f32[2,9,16,128]{3,2,1,0:T(8,128)S(1)} %get-tuple-element.50), channel_id=1, source_target_pairs={{0,8},{2,10},{4,12},{6,14},{8,0},{10,2},{12,4},{14,6},{16,24},{18,... | collective-permute-start | bytes 442376 | tf_op jit(solution)/shard_map/ppermute | solution.py:251
  29.1 8.7 %collective-permute-start.13 = (f32[9,16,128]{2,1,0:T(8,128)S(1)}, f32[9,16,128]{2,1,0:T(8,128)S(1)}, u32[]{:S(2)}, u32[]{:S(2)}) collective-permute-start(f32[9,16,128]{2,1,0:T(8,128)S(1)} %get-tuple-element.53), channel_id=1, source_target_pairs={{0,4},{2,6},{4,0},{6,2},{8,12},{10,14},{12,8},{14,10},{16,20},{18,... | collective-permute-start | bytes 221192 | tf_op jit(solution)/shard_map/ppermute | solution.py:251
  29.5 8.4 %collective-permute-start.14 = (f32[9,16,128]{2,1,0:T(8,128)S(1)}, f32[9,16,128]{2,1,0:T(8,128)S(1)}, u32[]{:S(2)}, u32[]{:S(2)}) collective-permute-start(f32[9,16,128]{2,1,0:T(8,128)S(1)} %get-tuple-element.54), channel_id=1, source_target_pairs={{0,12},{2,14},{4,8},{6,10},{8,4},{10,6},{12,0},{14,2},{16,28},{18,... | collective-permute-start | bytes 221192 | tf_op jit(solution)/shard_map/ppermute | solution.py:251
  30.6 8.6 %collective-permute-start.15 = (f32[9,16,128]{2,1,0:T(8,128)S(1)}, f32[9,16,128]{2,1,0:T(8,128)S(1)}, u32[]{:S(2)}, u32[]{:S(2)}) collective-permute-start(f32[9,16,128]{2,1,0:T(8,128)S(1)} %get-tuple-element.55), channel_id=1, source_target_pairs={{0,20},{2,22},{4,16},{6,18},{8,28},{10,30},{12,24},{14,26},{16,4},... | collective-permute-start | bytes 221192 | tf_op jit(solution)/shard_map/ppermute | solution.py:251
  33.9 7.1 %collective-permute-start.16 = (f32[9,16,128]{2,1,0:T(8,128)S(1)}, f32[9,16,128]{2,1,0:T(8,128)S(1)}, u32[]{:S(2)}, u32[]{:S(2)}) collective-permute-start(f32[9,16,128]{2,1,0:T(8,128)S(1)} %get-tuple-element.56), channel_id=1, source_target_pairs={{0,28},{2,30},{4,24},{6,26},{8,20},{10,22},{12,16},{14,18},{16,12}... | collective-permute-start | bytes 221192 | tf_op jit(solution)/shard_map/ppermute | solution.py:251
  35.8 6.9 %copy-start = (f32[4,16,2304]{2,1,0:T(8,128)S(1)}, f32[4,16,2304]{2,1,0:T(8,128)}, u32[]{:S(2)}) copy-start(f32[4,16,2304]{2,1,0:T(8,128)} %bank_ref.1) | copy-start | bytes 1769476
  35.8 6.8 %collective-permute-start.11 = (f32[9,16,128]{2,1,0:T(8,128)S(1)}, f32[9,16,128]{2,1,0:T(8,128)S(1)}, u32[]{:S(2)}, u32[]{:S(2)}) collective-permute-start(f32[9,16,128]{2,1,0:T(8,128)S(1)} %get-tuple-element.52), channel_id=1, source_target_pairs={{0,16},{2,18},{4,20},{6,22},{8,24},{10,26},{12,28},{14,30},{16,0},... | collective-permute-start | bytes 221192 | tf_op jit(solution)/shard_map/ppermute | solution.py:251
  37.8 4.9 %collective-permute-start.18 = (f32[16,128]{1,0:T(8,128)S(1)}, f32[16,128]{1,0:T(8,128)S(1)}, u32[]{:S(2)}, u32[]{:S(2)}) collective-permute-start(f32[16,128]{1,0:T(8,128)S(1)} %shard_map.64), channel_id=1, source_target_pairs={{1,0},{0,1},{3,2},{2,3},{5,4},{4,5},{7,6},{6,7},{9,8},{8,9},{11,10... | collective-permute-start | bytes 24584 | tf_op jit(solution)/shard_map/ppermute | solution.py:251
  41.0 2.0 %collective-permute-start.17 = (f32[9,16,128]{2,1,0:T(8,128)S(1)}, f32[9,16,128]{2,1,0:T(8,128)S(1)}, u32[]{:S(2)}, u32[]{:S(2)}) collective-permute-start(f32[9,16,128]{2,1,0:T(8,128)S(1)} %shard_map.63.got_own), channel_id=1, source_target_pairs={{1,0},{0,1},{3,2},{2,3},{5,4},{4,5},{7,6},{6,7},{9,8},{8,9},{11,10... | collective-permute-start | bytes 221192 | tf_op jit(solution)/shard_map/ppermute | solution.py:251
  42.7 1.3 %collective-permute-start.12 = (f32[9,16,128]{2,1,0:T(8,128)S(1)}, f32[9,16,128]{2,1,0:T(8,128)S(1)}, u32[]{:S(2)}, u32[]{:S(2)}) collective-permute-start(f32[9,16,128]{2,1,0:T(8,128)S(1)} %shard_map.62.kept_own), channel_id=1, source_target_pairs={{1,0},{0,1},{3,2},{2,3},{5,4},{4,5},{7,6},{6,7},{9,8},{8,9},{11,10... | collective-permute-start | bytes 221192 | tf_op jit(solution)/shard_map/ppermute | solution.py:251

commit v4 on v3

--- a/solution.py
+++ b/solution.py
@@ -108,6 +108,21 @@
     return product(lefts[0][role], lefts[1][role], rights[other], half)
 
 
+def mul_two(lefts, role, first, second):
+    half = first.shape[1] // 2
+    high, low = lefts[0][role], lefts[1][role]
+    lows = jnp.dot(
+        low,
+        jnp.concatenate([first[:, :half], second[:, :half]], axis=1),
+        preferred_element_type=F32,
+    )
+    sums = []
+    for right_one, rest in ((first, lows[:, :half]), (second, lows[:, half:])):
+        both = jnp.dot(high, right_one, preferred_element_type=F32)
+        sums.append(both[:, :half] + both[:, half:] + rest)
+    return sums
+
+
 def first_body(f_own, f_yn, g_own, g_xn, mid, side, lh, ll, rt):
     _, _, x, y = place()
     left(g_own, lh.at[0], ll.at[0])
@@ -155,8 +170,9 @@
     left(g_dg, lh_far.at[0], ll_far.at[0])
     right(f_dg, rt_far.at[0])
     lefts, lefts_yn, lefts_far = (lh, ll), (lh_yn, ll_yn), (lh_far, ll_far)
-    mid[...] = mid_in[...] + mul(lefts_far, 0, rt_far, 0)
-    side[x] = side_in[x] + mul(lefts_far, 0, rt, 1)
+    with_far, with_yn = mul_two(lefts_far, 0, rt_far[0], rt[1])
+    mid[...] = mid_in[...] + with_far
+    side[x] = side_in[x] + with_yn
     side[1 - x] = side_in[1 - x] + mul(lefts_yn, 0, rt_far, 0)
 
     @pl.when(x == y)
@@ -285,11 +301,16 @@
     g_xn = send(g_send, over_x)
 
     def others(value):
-        return [send(value, [((c + s) % cores, c) for c in range(cores)], "narrow") for s in range(1, cores)]
+        return [
+            send(value, [((c + s) % cores, c) for c in range(cores)], "narrow")
+            for s in range(1, cores)
+        ]
 
     every_mix = jnp.stack([mix] + others(mix))
     samples = every_mix.shape[0]
-    mixed, scale = call(mix_body, (shape(samples, *bank.shape[1:]), shape(samples, owned, 128)), "vv")(every_mix, bank)
+    mixed, scale = call(
+        mix_body, (shape(samples, *bank.shape[1:]), shape(samples, owned, 128)), "vv"
+    )(every_mix, bank)
     f_xn = send(f_keep, over_x)
     g_yn = send(g_keep, over_y)
     f_dg = send(f_yn, over_x)
@@ -318,10 +339,17 @@
         first_body, (mids, sides, lefts(2), lefts(2), rights(2)), "vvvv", flops=3 * pair
     )(f_keep, f_yn, g_keep, g_xn)
     mid, side, *more = call(
-        functools.partial(near_body, groups), (mids, sides, lefts(1), lefts(1), rights(2)), "v" * 9, flops=4 * pair
+        functools.partial(near_body, groups),
+        (mids, sides, lefts(1), lefts(1), rights(2)),
+        "v" * 9,
+        flops=4 * pair,
     )(f_xn, g_yn, f_even, f_odd, mid, side, lh, ll, rt)
     mid, side, rt_far = call(
-        far_body, (mids, sides, rights(1)), "v" * 10, flops=5 * pair, scratch=[pltpu.VMEM(lefts(1).shape, BF16)] * 2
+        far_body,
+        (mids, sides, rights(1)),
+        "v" * 10,
+        flops=5 * pair,
+        scratch=[pltpu.VMEM(lefts(1).shape, BF16)] * 2,
     )(f_dg, g_dg, mid, side, lh, ll, rt, *more)
     piece = shape(9, owned, half_in)
     stack = shape(groups // 2, *piece.shape)

time: 45.2 us -> 45.2 us (level)
  no operation moved by 1% of the time
where the time goes in v4:
time: 45.2 us; the launch traced here: 45.1 us
  starting transfers between devices  23 us (51%)
  waiting for transfers between devices  13.6 us (30%)
  Pallas kernels  6.56 us (15%)
  local copies, waits for them, and re-layouts  1.11 us (2%)
  between operations  0.82 us (2%)
    ppermute x19, starting transfers between devices, send(): return lax.ppermute(value, axes, pairs)  23 us
    ppermute x19, waiting for transfers between devices, send(): return lax.ppermute(value, axes, pairs)  13.6 us
    pallas_call x1, Pallas kernels, local(): call(functools.partial(near_body, groups), (mids, sides, lefts(1), lefts(...  1.47 us
    pallas_call x1, Pallas kernels, local(): call(far_body, (mids, sides, rights(1)), 'v' * 10, flops=5 * pair, scratc...  1.15 us
    pallas_call x1, Pallas kernels, local(): call(first_body, (mids, sides, lefts(2), lefts(2), rights(2)), 'vvvv', fl...  1.11 us
    unnamed x8, local copies, waits for them, and re-layouts  1.11 us
    pallas_call x1, Pallas kernels, local(): call(final_body, shape(*bank.shape), 'v' * 7, ANY_SPEC, scratch=(pltpu.VM...  1.11 us
  transfers between devices with their start and end apart: 19, of which 10 were waited for; matrix products, arithmetic and copies ran while one was open for 0% of the time, Pallas kernels for 11%

profile of v4, /device:TPU:0, one launch (start us, length us, event | category | flops | bytes accessed | tf_op | source)
XLA Modules:
  0.0 45.1 jit_solution(16143696609694237115)
XLA Ops:
  0.0 1.1 %copy-done.3 = f32[1,1,512,256]{3,2,1,0:T(8,128)S(1)} copy-done((f32[1,1,512,256]{3,2,1,0:T(8,128)S(1)}, f32[1,1,512,256]{3,2,1,0:T(8,128)}, u32[]{:S(2)}) %copy-start.3) | copy-done | bytes 524312
  1.1 3.1 %collective-permute-start.3 = (f32[512,128]{1,0:T(8,128)S(1)}, f32[512,128]{1,0:T(8,128)S(1)}, u32[]{:S(2)}, u32[]{:S(2)}) collective-permute-start(f32[512,128]{1,0:T(8,128)S(1)} %get-tuple-element.33), channel_id=1, source_target_pairs={{0,4},{2,6},{4,0},{6,2},{8,12},{10,14},{12,8},{14,10},{16,20},{18,... | collective-permute-start | bytes 786440 | tf_op jit(solution)/shard_map/ppermute | solution.py:267
  4.4 1.6 %collective-permute-start.5 = (f32[128,512]{1,0:T(8,128)S(1)}, f32[128,512]{1,0:T(8,128)S(1)}, u32[]{:S(2)}, u32[]{:S(2)}) collective-permute-start(f32[128,512]{1,0:T(8,128)S(1)} %get-tuple-element.34.after_ref), channel_id=1, source_target_pairs={{0,2},{2,0},{4,6},{6,4},{8,10},{10,8},{12,14},{14,12},{16,18},{18,... | collective-permute-start | bytes 786440 | tf_op jit(solution)/shard_map/ppermute | solution.py:267
  6.5 4.8 %collective-permute-done.3.f_yn = f32[512,128]{1,0:T(8,128)S(1)} collective-permute-done((f32[512,128]{1,0:T(8,128)S(1)}, f32[512,128]{1,0:T(8,128)S(1)}, u32[]{:S(2)}, u32[]{:S(2)}) %collective-permute-start.3) | collective-permute-done | bytes 262176 | tf_op jit(solution)/shard_map/ppermute | solution.py:267
  11.4 2.1 %collective-permute-start.8 = (f32[512,128]{1,0:T(8,128)S(1)}, f32[512,128]{1,0:T(8,128)S(1)}, u32[]{:S(2)}, u32[]{:S(2)}) collective-permute-start(f32[512,128]{1,0:T(8,128)S(1)} %broadcast_select_fusion), channel_id=1, source_target_pairs={{0,8},{2,10},{4,12},{6,14},{8,0},{10,2},{12,4},{14,6},{16,24},{18,... | collective-permute-start | bytes 786440 | tf_op jit(solution)/shard_map/ppermute | solution.py:267
  13.6 1.5 %collective-permute-start.4 = (f32[512,128]{1,0:T(8,128)S(1)}, f32[512,128]{1,0:T(8,128)S(1)}, u32[]{:S(2)}, u32[]{:S(2)}) collective-permute-start(f32[512,128]{1,0:T(8,128)S(1)} %collective-permute-done.3.f_yn), channel_id=1, source_target_pairs={{0,2},{2,0},{4,6},{6,4},{8,10},{10,8},{12,14},{14,12},{16,18},{18,... | collective-permute-start | bytes 786440 | tf_op jit(solution)/shard_map/ppermute | solution.py:267
  15.1 1.0 %collective-permute-done.g_yn = f32[128,512]{1,0:T(8,128)S(1)} collective-permute-done((f32[128,512]{1,0:T(8,128)S(1)}, f32[128,512]{1,0:T(8,128)S(1)}, u32[]{:S(2)}, u32[]{:S(2)}) %collective-permute-start) | collective-permute-done | bytes 262176 | tf_op jit(solution)/shard_map/ppermute | solution.py:267
  16.1 1.7 %collective-permute-start.6 = (f32[128,512]{1,0:T(8,128)S(1)}, f32[128,512]{1,0:T(8,128)S(1)}, u32[]{:S(2)}, u32[]{:S(2)}) collective-permute-start(f32[128,512]{1,0:T(8,128)S(1)} %collective-permute-done.5.g_xn), channel_id=1, source_target_pairs={{0,4},{2,6},{4,0},{6,2},{8,12},{10,14},{12,8},{14,10},{16,20},{18,... | collective-permute-start | bytes 786440 | tf_op jit(solution)/shard_map/ppermute | solution.py:267
  17.9 1.2 %collective-permute-done.7.f_xn = f32[512,128]{1,0:T(8,128)S(1)} collective-permute-done((f32[512,128]{1,0:T(8,128)S(1)}, f32[512,128]{1,0:T(8,128)S(1)}, u32[]{:S(2)}, u32[]{:S(2)}) %collective-permute-start.7) | collective-permute-done | bytes 262176 | tf_op jit(solution)/shard_map/ppermute | solution.py:267
  19.1 1.8 %collective-permute-start.1 = (f32[128,512]{1,0:T(8,128)S(1)}, f32[128,512]{1,0:T(8,128)S(1)}, u32[]{:S(2)}, u32[]{:S(2)}) collective-permute-start(f32[128,512]{1,0:T(8,128)S(1)} %broadcast_select_fusion.1), channel_id=1, source_target_pairs={{0,8},{2,10},{4,12},{6,14},{8,0},{10,2},{12,4},{14,6},{16,24},{18,... | collective-permute-start | bytes 786440 | tf_op jit(solution)/shard_map/ppermute | solution.py:267
  20.8 1.1 %shard_map.57 = (f32[384,128]{1,0:T(8,128)S(1)}, f32[2,384,128]{2,1,0:T(8,128)S(1)}, bf16[2,384,512]{2,1,0:T(8,128)(2,1)S(1)}, bf16[2,384,512]{2,1,0:T(8,128)(2,1)S(1)}, bf16[2,512,256]{2,1,0:T(8,128)(2,1)S(1)}) custom-call(f32[512,128]{1,0:T(8,128)S(1)} %get-tuple-element.35.f_own, f32[512,128]{1,0:T(8,128)S(1)} %collective-permute-done.3.f_yn, ...), custom_call_target="tpu_custom_call" | custom-call | flops 452984832 | bytes 1048576 | tf_op jit(solution)/shard_map/pallas_call | solution.py:338
  22.0 1.5 %shard_map.58 = (f32[384,128]{1,0:T(8,128)S(1)}, f32[2,384,128]{2,1,0:T(8,128)S(1)}, bf16[1,384,512]{2,1,0:T(8,128)(2,1)S(1)}, bf16[1,384,512]{2,1,0:T(8,128)(2,1)S(1)}, bf16[2,512,256]{2,1,0:T(8,128)(2,1)S(1)}) custom-call(f32[512,128]{1,0:T(8,128)S(1)} %collective-permute-done.7.f_xn, f32[128,512]{1,0:T(8,128)S(1)} %collective-permute-done.g_yn, ...), custom_call_target="tpu_custom_call" | custom-call | flops 603979776 | bytes 1048576 | tf_op jit(solution)/shard_map/pallas_call | solution.py:341
  23.6 1.2 %shard_map.59 = (f32[384,128]{1,0:T(8,128)S(1)}, f32[2,384,128]{2,1,0:T(8,128)S(1)}, bf16[1,512,256]{2,1,0:T(8,128)(2,1)S(1)}) custom-call(f32[512,128]{1,0:T(8,128)S(1)} %collective-permute-done.4.f_dg, f32[128,512]{1,0:T(8,128)S(1)} %collective-permute-done.6.g_dg, f32[384,128]{1,0:T(8,128)S(1)} %get-tuple-element.41.mid_in, ...), custom_call_target="tpu_custom_call" | custom-call | flops 754974720 | bytes 1048576 | tf_op jit(solution)/shard_map/pallas_call | solution.py:347
  24.8 0.7 %collective-permute-done.1.g_even = f32[128,512]{1,0:T(8,128)S(1)} collective-permute-done((f32[128,512]{1,0:T(8,128)S(1)}, f32[128,512]{1,0:T(8,128)S(1)}, u32[]{:S(2)}, u32[]{:S(2)}) %collective-permute-start.1) | collective-permute-done | bytes 262176 | tf_op jit(solution)/shard_map/ppermute | solution.py:267
  26.1 3.0 %collective-permute-start.10 = (f32[2,9,16,128]{3,2,1,0:T(8,128)S(1)}, f32[2,9,16,128]{3,2,1,0:T(8,128)S(1)}, u32[]{:S(2)}, u32[]{:S(2)}) collective-permute-start(f32[2,9,16,128]{3,2,1,0:T(8,128)S(1)} %get-tuple-element.50), channel_id=1, source_target_pairs={{0,8},{2,10},{4,12},{6,14},{8,0},{10,2},{12,4},{14,6},{16,24},{18,... | collective-permute-start | bytes 442376 | tf_op jit(solution)/shard_map/ppermute | solution.py:267
  29.5 1.1 %collective-permute-start.14 = (f32[9,16,128]{2,1,0:T(8,128)S(1)}, f32[9,16,128]{2,1,0:T(8,128)S(1)}, u32[]{:S(2)}, u32[]{:S(2)}) collective-permute-start(f32[9,16,128]{2,1,0:T(8,128)S(1)} %get-tuple-element.54), channel_id=1, source_target_pairs={{0,12},{2,14},{4,8},{6,10},{8,4},{10,6},{12,0},{14,2},{16,28},{18,... | collective-permute-start | bytes 221192 | tf_op jit(solution)/shard_map/ppermute | solution.py:267
  30.6 3.3 %collective-permute-start.15 = (f32[9,16,128]{2,1,0:T(8,128)S(1)}, f32[9,16,128]{2,1,0:T(8,128)S(1)}, u32[]{:S(2)}, u32[]{:S(2)}) collective-permute-start(f32[9,16,128]{2,1,0:T(8,128)S(1)} %get-tuple-element.55), channel_id=1, source_target_pairs={{0,20},{2,22},{4,16},{6,18},{8,28},{10,30},{12,24},{14,26},{16,4},... | collective-permute-start | bytes 221192 | tf_op jit(solution)/shard_map/ppermute | solution.py:267
  33.9 1.9 %collective-permute-start.16 = (f32[9,16,128]{2,1,0:T(8,128)S(1)}, f32[9,16,128]{2,1,0:T(8,128)S(1)}, u32[]{:S(2)}, u32[]{:S(2)}) collective-permute-start(f32[9,16,128]{2,1,0:T(8,128)S(1)} %get-tuple-element.56), channel_id=1, source_target_pairs={{0,28},{2,30},{4,24},{6,26},{8,20},{10,22},{12,16},{14,18},{16,12}... | collective-permute-start | bytes 221192 | tf_op jit(solution)/shard_map/ppermute | solution.py:267
  35.8 0.7 %collective-permute-start.11 = (f32[9,16,128]{2,1,0:T(8,128)S(1)}, f32[9,16,128]{2,1,0:T(8,128)S(1)}, u32[]{:S(2)}, u32[]{:S(2)}) collective-permute-start(f32[9,16,128]{2,1,0:T(8,128)S(1)} %get-tuple-element.52), channel_id=1, source_target_pairs={{0,16},{2,18},{4,20},{6,22},{8,24},{10,26},{12,28},{14,30},{16,0},... | collective-permute-start | bytes 221192 | tf_op jit(solution)/shard_map/ppermute | solution.py:267
  37.9 1.2 %collective-permute-done.15.refs_2_ = f32[9,16,128]{2,1,0:T(8,128)S(1)} collective-permute-done((f32[9,16,128]{2,1,0:T(8,128)S(1)}, f32[9,16,128]{2,1,0:T(8,128)S(1)}, u32[]{:S(2)}, u32[]{:S(2)}) %collective-permute-start.15) | collective-permute-done | bytes 73760 | tf_op jit(solution)/shard_map/ppermute | solution.py:267
  39.1 1.9 %collective-permute-done.16.refs_3_ = f32[9,16,128]{2,1,0:T(8,128)S(1)} collective-permute-done((f32[9,16,128]{2,1,0:T(8,128)S(1)}, f32[9,16,128]{2,1,0:T(8,128)S(1)}, u32[]{:S(2)}, u32[]{:S(2)}) %collective-permute-start.16) | collective-permute-done | bytes 73760 | tf_op jit(solution)/shard_map/ppermute | solution.py:267
  41.1 1.5 %collective-permute-done.11.refs_1_ = f32[9,16,128]{2,1,0:T(8,128)S(1)} collective-permute-done((f32[9,16,128]{2,1,0:T(8,128)S(1)}, f32[9,16,128]{2,1,0:T(8,128)S(1)}, u32[]{:S(2)}, u32[]{:S(2)}) %collective-permute-start.11) | collective-permute-done | bytes 73760 | tf_op jit(solution)/shard_map/ppermute | solution.py:267
  43.0 1.0 %collective-permute-done.12 = f32[9,16,128]{2,1,0:T(8,128)S(1)} collective-permute-done((f32[9,16,128]{2,1,0:T(8,128)S(1)}, f32[9,16,128]{2,1,0:T(8,128)S(1)}, u32[]{:S(2)}, u32[]{:S(2)}) %collective-permute-start.12) | collective-permute-done | bytes 73760 | tf_op jit(solution)/shard_map/ppermute | solution.py:267
  44.0 1.1 %shard_map.66 = f32[4,16,2304]{2,1,0:T(8,128)} custom-call(f32[9,16,128]{2,1,0:T(8,128)S(1)} %shard_map.62.kept_own, f32[1,9,16,128]{3,2,1,0:T(8,128)S(1)} %bitcast.6, f32[9,16,128]{2,1,0:T(8,128)S(1)} %shard_map.63.got_own, f32[1,9,16,128]{3,2,1,0:T(8,128)S(1)} %bitcast.5, f32[2,16,128]{2,1,0:T(8,128)S(1)} %pad_maximum_fusion.every_ref, ...), custom_call_target="tpu_custom_call" | custom-call | bytes 1048576 | tf_op jit(solution)/shard_map/pallas_call | solution.py:379
  (37 shorter events, 3.3 us)
Async XLA Ops:
  0.0 4.2 %copy-start.1 = (f32[1,1,512,256]{3,2,1,0:T(8,128)S(1)}, f32[1,1,512,256]{3,2,1,0:T(8,128)}, u32[]{:S(2)}) copy-start(f32[1,1,512,256]{3,2,1,0:T(8,128)} %g_ref.1) | copy-start | bytes 1572868
  0.0 1.1 %copy-start.3 = (f32[1,1,512,256]{3,2,1,0:T(8,128)S(1)}, f32[1,1,512,256]{3,2,1,0:T(8,128)}, u32[]{:S(2)}) copy-start(f32[1,1,512,256]{3,2,1,0:T(8,128)} %f_ref.1) | copy-start | bytes 1572868
  1.1 10.2 %collective-permute-start.3 = (f32[512,128]{1,0:T(8,128)S(1)}, f32[512,128]{1,0:T(8,128)S(1)}, u32[]{:S(2)}, u32[]{:S(2)}) collective-permute-start(f32[512,128]{1,0:T(8,128)S(1)} %get-tuple-element.33), channel_id=1, source_target_pairs={{0,4},{2,6},{4,0},{6,2},{8,12},{10,14},{12,8},{14,10},{16,20},{18,... | collective-permute-start | bytes 786440 | tf_op jit(solution)/shard_map/ppermute | solution.py:267
  4.4 9.2 %collective-permute-start.5 = (f32[128,512]{1,0:T(8,128)S(1)}, f32[128,512]{1,0:T(8,128)S(1)}, u32[]{:S(2)}, u32[]{:S(2)}) collective-permute-start(f32[128,512]{1,0:T(8,128)S(1)} %get-tuple-element.34.after_ref), channel_id=1, source_target_pairs={{0,2},{2,0},{4,6},{6,4},{8,10},{10,8},{12,14},{14,12},{16,18},{18,... | collective-permute-start | bytes 786440 | tf_op jit(solution)/shard_map/ppermute | solution.py:267
  6.0 10.2 %collective-permute-start = (f32[128,512]{1,0:T(8,128)S(1)}, f32[128,512]{1,0:T(8,128)S(1)}, u32[]{:S(2)}, u32[]{:S(2)}) collective-permute-start(f32[128,512]{1,0:T(8,128)S(1)} %get-tuple-element.32.g_own), channel_id=1, source_target_pairs={{0,4},{2,6},{4,0},{6,2},{8,12},{10,14},{12,8},{14,10},{16,20},{18,... | collective-permute-start | bytes 786440 | tf_op jit(solution)/shard_map/ppermute | solution.py:267
  6.5 12.6 %collective-permute-start.7 = (f32[512,128]{1,0:T(8,128)S(1)}, f32[512,128]{1,0:T(8,128)S(1)}, u32[]{:S(2)}, u32[]{:S(2)}) collective-permute-start(f32[512,128]{1,0:T(8,128)S(1)} %get-tuple-element.35.f_own), channel_id=1, source_target_pairs={{0,2},{2,0},{4,6},{6,4},{8,10},{10,8},{12,14},{14,12},{16,18},{18,... | collective-permute-start | bytes 786440 | tf_op jit(solution)/shard_map/ppermute | solution.py:267
  11.4 9.5 %collective-permute-start.8 = (f32[512,128]{1,0:T(8,128)S(1)}, f32[512,128]{1,0:T(8,128)S(1)}, u32[]{:S(2)}, u32[]{:S(2)}) collective-permute-start(f32[512,128]{1,0:T(8,128)S(1)} %broadcast_select_fusion), channel_id=1, source_target_pairs={{0,8},{2,10},{4,12},{6,14},{8,0},{10,2},{12,4},{14,6},{16,24},{18,... | collective-permute-start | bytes 786440 | tf_op jit(solution)/shard_map/ppermute | solution.py:267
  13.5 8.4 %collective-permute-start.9 = (f32[512,128]{1,0:T(8,128)S(1)}, f32[512,128]{1,0:T(8,128)S(1)}, u32[]{:S(2)}, u32[]{:S(2)}) collective-permute-start(f32[512,128]{1,0:T(8,128)S(1)} %broadcast_select_fusion), channel_id=1, source_target_pairs={{0,1},{1,0},{2,3},{3,2},{4,5},{5,4},{6,7},{7,6},{8,16},{9,17},{10,... | collective-permute-start | bytes 786440 | tf_op jit(solution)/shard_map/ppermute | solution.py:267
  13.6 9.8 %collective-permute-start.4 = (f32[512,128]{1,0:T(8,128)S(1)}, f32[512,128]{1,0:T(8,128)S(1)}, u32[]{:S(2)}, u32[]{:S(2)}) collective-permute-start(f32[512,128]{1,0:T(8,128)S(1)} %collective-permute-done.3.f_yn), channel_id=1, source_target_pairs={{0,2},{2,0},{4,6},{6,4},{8,10},{10,8},{12,14},{14,12},{16,18},{18,... | collective-permute-start | bytes 786440 | tf_op jit(solution)/shard_map/ppermute | solution.py:267
  16.1 7.5 %collective-permute-start.6 = (f32[128,512]{1,0:T(8,128)S(1)}, f32[128,512]{1,0:T(8,128)S(1)}, u32[]{:S(2)}, u32[]{:S(2)}) collective-permute-start(f32[128,512]{1,0:T(8,128)S(1)} %collective-permute-done.5.g_xn), channel_id=1, source_target_pairs={{0,4},{2,6},{4,0},{6,2},{8,12},{10,14},{12,8},{14,10},{16,20},{18,... | collective-permute-start | bytes 786440 | tf_op jit(solution)/shard_map/ppermute | solution.py:267
  19.1 6.4 %collective-permute-start.1 = (f32[128,512]{1,0:T(8,128)S(1)}, f32[128,512]{1,0:T(8,128)S(1)}, u32[]{:S(2)}, u32[]{:S(2)}) collective-permute-start(f32[128,512]{1,0:T(8,128)S(1)} %broadcast_select_fusion.1), channel_id=1, source_target_pairs={{0,8},{2,10},{4,12},{6,14},{8,0},{10,2},{12,4},{14,6},{16,24},{18,... | collective-permute-start | bytes 786440 | tf_op jit(solution)/shard_map/ppermute | solution.py:267
  20.8 4.6 %collective-permute-start.2 = (f32[128,512]{1,0:T(8,128)S(1)}, f32[128,512]{1,0:T(8,128)S(1)}, u32[]{:S(2)}, u32[]{:S(2)}) collective-permute-start(f32[128,512]{1,0:T(8,128)S(1)} %broadcast_select_fusion.1), channel_id=1, source_target_pairs={{0,1},{1,0},{2,3},{3,2},{4,5},{5,4},{6,7},{7,6},{8,16},{9,17},{10,... | collective-permute-start | bytes 786440 | tf_op jit(solution)/shard_map/ppermute | solution.py:267
  25.4 11.8 %copy-start.2 = (s32[16,4]{0,1:T(4,128)S(1)}, s32[16,4]{0,1:T(4,128)}, u32[]{:S(2)}) copy-start(s32[16,4]{0,1:T(4,128)} %param.8) | copy-start | bytes 772
  26.1 9.7 %collective-permute-start.10 = (f32[2,9,16,128]{3,2,1,0:T(8,128)S(1)}, f32[2,9,16,128]{3,2,1,0:T(8,128)S(1)}, u32[]{:S(2)}, u32[]{:S(2)}) collective-permute-start(f32[2,9,16,128]{3,2,1,0:T(8,128)S(1)} %get-tuple-element.50), channel_id=1, source_target_pairs={{0,8},{2,10},{4,12},{6,14},{8,0},{10,2},{12,4},{14,6},{16,24},{18,... | collective-permute-start | bytes 442376 | tf_op jit(solution)/shard_map/ppermute | solution.py:267
  29.1 8.7 %collective-permute-start.13 = (f32[9,16,128]{2,1,0:T(8,128)S(1)}, f32[9,16,128]{2,1,0:T(8,128)S(1)}, u32[]{:S(2)}, u32[]{:S(2)}) collective-permute-start(f32[9,16,128]{2,1,0:T(8,128)S(1)} %get-tuple-element.53), channel_id=1, source_target_pairs={{0,4},{2,6},{4,0},{6,2},{8,12},{10,14},{12,8},{14,10},{16,20},{18,... | collective-permute-start | bytes 221192 | tf_op jit(solution)/shard_map/ppermute | solution.py:267
  29.5 8.4 %collective-permute-start.14 = (f32[9,16,128]{2,1,0:T(8,128)S(1)}, f32[9,16,128]{2,1,0:T(8,128)S(1)}, u32[]{:S(2)}, u32[]{:S(2)}) collective-permute-start(f32[9,16,128]{2,1,0:T(8,128)S(1)} %get-tuple-element.54), channel_id=1, source_target_pairs={{0,12},{2,14},{4,8},{6,10},{8,4},{10,6},{12,0},{14,2},{16,28},{18,... | collective-permute-start | bytes 221192 | tf_op jit(solution)/shard_map/ppermute | solution.py:267
  30.6 8.5 %collective-permute-start.15 = (f32[9,16,128]{2,1,0:T(8,128)S(1)}, f32[9,16,128]{2,1,0:T(8,128)S(1)}, u32[]{:S(2)}, u32[]{:S(2)}) collective-permute-start(f32[9,16,128]{2,1,0:T(8,128)S(1)} %get-tuple-element.55), channel_id=1, source_target_pairs={{0,20},{2,22},{4,16},{6,18},{8,28},{10,30},{12,24},{14,26},{16,4},... | collective-permute-start | bytes 221192 | tf_op jit(solution)/shard_map/ppermute | solution.py:267
  33.9 7.1 %collective-permute-start.16 = (f32[9,16,128]{2,1,0:T(8,128)S(1)}, f32[9,16,128]{2,1,0:T(8,128)S(1)}, u32[]{:S(2)}, u32[]{:S(2)}) collective-permute-start(f32[9,16,128]{2,1,0:T(8,128)S(1)} %get-tuple-element.56), channel_id=1, source_target_pairs={{0,28},{2,30},{4,24},{6,26},{8,20},{10,22},{12,16},{14,18},{16,12}... | collective-permute-start | bytes 221192 | tf_op jit(solution)/shard_map/ppermute | solution.py:267
  35.8 6.9 %copy-start = (f32[4,16,2304]{2,1,0:T(8,128)S(1)}, f32[4,16,2304]{2,1,0:T(8,128)}, u32[]{:S(2)}) copy-start(f32[4,16,2304]{2,1,0:T(8,128)} %bank_ref.1) | copy-start | bytes 1769476
  35.8 6.8 %collective-permute-start.11 = (f32[9,16,128]{2,1,0:T(8,128)S(1)}, f32[9,16,128]{2,1,0:T(8,128)S(1)}, u32[]{:S(2)}, u32[]{:S(2)}) collective-permute-start(f32[9,16,128]{2,1,0:T(8,128)S(1)} %get-tuple-element.52), channel_id=1, source_target_pairs={{0,16},{2,18},{4,20},{6,22},{8,24},{10,26},{12,28},{14,30},{16,0},... | collective-permute-start | bytes 221192 | tf_op jit(solution)/shard_map/ppermute | solution.py:267
  37.8 4.9 %collective-permute-start.18 = (f32[16,128]{1,0:T(8,128)S(1)}, f32[16,128]{1,0:T(8,128)S(1)}, u32[]{:S(2)}, u32[]{:S(2)}) collective-permute-start(f32[16,128]{1,0:T(8,128)S(1)} %shard_map.64), channel_id=1, source_target_pairs={{1,0},{0,1},{3,2},{2,3},{5,4},{4,5},{7,6},{6,7},{9,8},{8,9},{11,10... | collective-permute-start | bytes 24584 | tf_op jit(solution)/shard_map/ppermute | solution.py:267
  41.0 2.0 %collective-permute-start.17 = (f32[9,16,128]{2,1,0:T(8,128)S(1)}, f32[9,16,128]{2,1,0:T(8,128)S(1)}, u32[]{:S(2)}, u32[]{:S(2)}) collective-permute-start(f32[9,16,128]{2,1,0:T(8,128)S(1)} %shard_map.63.got_own), channel_id=1, source_target_pairs={{1,0},{0,1},{3,2},{2,3},{5,4},{4,5},{7,6},{6,7},{9,8},{8,9},{11,10... | collective-permute-start | bytes 221192 | tf_op jit(solution)/shard_map/ppermute | solution.py:267
  42.7 1.3 %collective-permute-start.12 = (f32[9,16,128]{2,1,0:T(8,128)S(1)}, f32[9,16,128]{2,1,0:T(8,128)S(1)}, u32[]{:S(2)}, u32[]{:S(2)}) collective-permute-start(f32[9,16,128]{2,1,0:T(8,128)S(1)} %shard_map.62.kept_own), channel_id=1, source_target_pairs={{1,0},{0,1},{3,2},{2,3},{5,4},{4,5},{7,6},{6,7},{9,8},{8,9},{11,10... | collective-permute-start | bytes 221192 | tf_op jit(solution)/shard_map/ppermute | solution.py:267
